TPU v7x, 512 devices: a whole 4x8x8 slice. The times are simulated.
512 devices in a mesh: rep: 32 (over z, y_hi), sp: 16 (over y_lo, x, core).
Axes of the slice: x: 4, y: 8 (y_hi: 4, y_lo: 2; y = y_hi * 2 + y_lo), z: 8, core: 2. Of those that a mesh axis runs over, the one named last changes fastest.
Arguments:
- queries: bfloat16 [32, 3072, 2048], P('rep', 'sp'), may hold values from -13 to 13
- key_rows: bfloat16 [32, 3072, 2048], P('rep', 'sp'), may hold values from -13 to 13
- values: bfloat16 [32, 3072, 2048], P('rep', 'sp'), may hold values from -6 to 6
- out_grad: bfloat16 [32, 3072, 3072], P('rep', 'sp'), may hold values from -6 to 6
- clip_count: int32 [32], P('rep'), may hold values from 1 to 3, as said below
- clip_lengths: int32 [32, 3], P('rep'), may hold values from 0 to 3072, as said below
- adapter_in: float32 [2048, 128], P('sp'), may hold values from -4 to 4
- adapter_out: float32 [128, 3072], P('sp'), may hold values from -4 to 4
- moment_in: float32 [2048, 128], P('sp'), may hold values from -3 to 3
- square_in: float32 [2048, 128], P('sp'), may hold values from 0.05 to 2
- moment_out: float32 [128, 3072], P('sp'), may hold values from -3 to 3
- square_out: float32 [128, 3072], P('sp'), may hold values from 0.05 to 2
Outputs:
- momentum_in: float32 [2048, 128], P('sp')
- variance_in: float32 [2048, 128], P('sp')
- update_in: float32 [2048, 128], P('sp')
- momentum_out: float32 [128, 3072], P('sp')
- variance_out: float32 [128, 3072], P('sp')
- update_out: float32 [128, 3072], P('sp')
Inputs may be any that keep to these rules, and one draw needn't show every extreme that they name: `clip_count`: in every draw some replica has 1 clip and some replica has 3. `clip_lengths`: each entry is a multiple of 384; entries at or beyond a replica's clip count are 0, the others 384 or more; the entries of a replica sum to at most 3072, and in every draw some replica holds a single clip of exactly 3072.
All inputs are finite; a program needn't handle non-finite values.
Results may differ from a plain program's by a relative error of at most 0.0017.
Values may be sent and summed in bfloat16 or wider, within the bound.
A program may use at most 64 MiB of HBM per device.

v0:
```python
import math

import jax
import jax.numpy as jnp
from jax import lax
from jax.sharding import PartitionSpec as P

HD = 128
MAX_CLIPS = 3


first_rate = 0.9
second_rate = 0.999
adam_steps = 100.0
adam_epsilon = 1e-08
decay_rate = 0.1


def laid_out(blocks, dim):
    shape = list(blocks.shape[1:])
    shape[dim] *= blocks.shape[0]
    return jnp.moveaxis(blocks, 0, dim).reshape(shape)


def gather_packed(arrays, axis, dims):
    ravelled = jnp.concatenate([a.reshape(-1) for a in arrays])
    lines, at, done = (lax.all_gather(ravelled, axis), 0, [])
    for a, dim in zip(arrays, dims):
        blocks = lines[:, at : at + a.size].reshape(-1, *a.shape)
        done.append(laid_out(blocks, dim))
        at += a.size
    return tuple(done)


def cut_along(array, dim, peers):
    shape = array.shape
    blocks = array.reshape(*shape[:dim], peers, shape[dim] // peers, *shape[dim + 1 :])
    return jnp.moveaxis(blocks, dim, 0)


def sum_packed(arrays, axis, dims):
    peers = lax.axis_size(axis)
    blocks = [cut_along(a, dim, peers) for a, dim in zip(arrays, dims)]
    lines = jnp.concatenate([b.reshape(peers, -1) for b in blocks], axis=1)
    extent = max(16, -(-lines.shape[1] // 1024) * 8)
    lines = jnp.pad(lines, ((0, 0), (0, extent * 128 - lines.shape[1]))).reshape(-1, 128)
    ravelled, at, done = (lax.psum_scatter(lines, axis, tiled=True).reshape(-1), 0, [])
    for b in blocks:
        part = b[0]
        done.append(ravelled[at : at + part.size].reshape(part.shape))
        at += part.size
    return tuple(done)


def padded_to(lines, peers):
    spare = -lines.shape[0] % peers
    if not spare:
        return lines
    return jnp.concatenate([lines, jnp.zeros((spare, *lines.shape[1:]), lines.dtype)])


def sent_to_all(array, axis):
    peers = lax.axis_size(axis)
    return lax.all_to_all(
        jnp.broadcast_to(array[None], (peers, *array.shape)), axis, 0, 0, tiled=True
    )


def gathered_copies(array, axis, dim):
    return laid_out(sent_to_all(array, axis), dim)


def summed_on_arrival(array, axis, dim):
    blocks = cut_along(array, dim, lax.axis_size(axis))
    arrived = lax.all_to_all(blocks, axis, split_axis=0, concat_axis=0, tiled=True)
    return arrived.sum(axis=0)


def total_of(array, axes):
    padded = padded_to(array, lax.axis_size(axes))
    whole = gathered_copies(summed_on_arrival(padded, axes, 0), axes, 0)
    return lax.slice_in_dim(whole, 0, len(array)).reshape(array.shape)


def packed_total(arrays, axis):
    ends = [0]
    for a in arrays:
        ends.append(ends[-1] + a.size)
    total = total_of(jnp.concatenate([a.ravel() for a in arrays]), axis)
    return tuple((total[b:e].reshape(a.shape) for a, b, e in zip(arrays, ends, ends[1:])))


def segment_ids(count, lengths, positions):
    active = (jnp.arange(lengths.shape[0], dtype=jnp.int32) < count).astype(lengths.dtype)
    ends = jnp.cumsum(lengths * active)
    return jnp.sum((positions[:, None] >= ends[None, :]).astype(jnp.int32), axis=1)


def adamw(param, grad, moment, square):
    momentum = first_rate * moment + (1.0 - first_rate) * grad
    variance = second_rate * square + (1.0 - second_rate) * grad * grad
    first_hat = momentum / (1.0 - first_rate**adam_steps)
    second_hat = variance / (1.0 - second_rate**adam_steps)
    update = first_hat / (jnp.sqrt(second_hat) + adam_epsilon) + decay_rate * param
    return (momentum, variance, update)


def contract_rows(left, right):
    return lax.dot_general(
        left, right, (((0,), (0,)), ((), ())), preferred_element_type=jnp.float32
    )


def per_device(
    queries,
    key_rows,
    values,
    out_grad,
    clip_count,
    clip_lengths,
    adapter_in,
    adapter_out,
    moment_in,
    square_in,
    moment_out,
    square_out,
):
    tok_dev = queries.shape[1]
    inner = queries.shape[2]
    rank = adapter_in.shape[1]
    groups = lax.axis_size("sp")
    tokens = tok_dev * groups
    heads = inner // HD
    head_share = heads // groups
    positions = jnp.arange(tokens, dtype=jnp.int32)
    segment = segment_ids(clip_count[0], clip_lengths[0], positions)
    segment_mine = lax.dynamic_slice_in_dim(segment, lax.axis_index("sp") * tok_dev, tok_dev)
    live = (segment_mine < MAX_CLIPS).astype(out_grad.dtype)
    grad_live = out_grad[0] * live[:, None]
    block = math.gcd(512, tokens)
    blocks = tokens // block

    def attend_head(query_head, key_head, value_head):

        def one_block(pair):
            query_block, segment_block = pair
            scores = lax.dot_general(
                query_block, key_head, (((1,), (1,)), ((), ())), preferred_element_type=jnp.float32
            ) * HD ** (-0.5)
            allowed = segment_block[:, None] == segment[None, :]
            highest = jnp.max(jnp.where(allowed, scores, -jnp.inf), axis=1, keepdims=True)
            exponent = jnp.exp(jnp.where(allowed, scores - highest, -jnp.inf))
            row_total = jnp.sum(exponent, axis=1, keepdims=True)
            weights = exponent.astype(jnp.bfloat16)
            mixed = jnp.dot(weights, value_head, preferred_element_type=jnp.float32) / row_total
            return mixed.astype(jnp.bfloat16)

        result = lax.map(
            one_block, (query_head.reshape(blocks, block, HD), segment.reshape(blocks, block))
        )
        return result.reshape(tokens, HD)

    query_split = queries.reshape(tok_dev, groups, head_share, HD)
    key_split = key_rows.reshape(tok_dev, groups, head_share, HD)
    value_split = values.reshape(tok_dev, groups, head_share, HD)
    query_part = lax.all_to_all(query_split, "sp", split_axis=1, concat_axis=0, tiled=True)
    key_part = lax.all_to_all(key_split, "sp", split_axis=1, concat_axis=0, tiled=True)
    value_part = lax.all_to_all(value_split, "sp", split_axis=1, concat_axis=0, tiled=True)
    per_head = jax.vmap(attend_head, in_axes=1, out_axes=1)
    mixed = per_head(query_part[:, 0], key_part[:, 0], value_part[:, 0])[:, None]
    returned = lax.all_to_all(mixed, "sp", split_axis=0, concat_axis=1, tiled=True)
    attended = returned.reshape(tok_dev, inner)
    inner_all, outer_all = gather_packed(
        (adapter_in.astype(jnp.bfloat16), adapter_out.astype(jnp.bfloat16)), "sp", (0, 0)
    )
    adapted = (
        jnp.dot(attended, inner_all, preferred_element_type=jnp.float32) * inner ** (-0.5)
    ).astype(jnp.bfloat16)
    slopes = (
        lax.dot_general(
            grad_live, outer_all, (((1,), (1,)), ((), ())), preferred_element_type=jnp.float32
        )
        * rank ** (-0.5)
    ).astype(jnp.bfloat16)
    term_in = contract_rows(attended, slopes) * inner ** (-0.5)
    term_out = contract_rows(adapted, grad_live) * rank ** (-0.5)
    grad_in, grad_out = sum_packed((term_in, term_out), "sp", (0, 0))
    grad_in, grad_out = packed_total((grad_in, grad_out), "rep")
    momentum_in, variance_in, update_in = adamw(adapter_in, grad_in, moment_in, square_in)
    momentum_out, variance_out, update_out = adamw(adapter_out, grad_out, moment_out, square_out)
    return (momentum_in, variance_in, update_in, momentum_out, variance_out, update_out)


def solution(mesh):
    placed = (
        P("rep", "sp", None),
        P("rep", "sp", None),
        P("rep", "sp", None),
        P("rep", "sp", None),
        P("rep"),
        P("rep", None),
        P("sp", None),
        P("sp", None),
        P("sp", None),
        P("sp", None),
        P("sp", None),
        P("sp", None),
    )
    return jax.shard_map(
        per_device,
        mesh=mesh,
        in_specs=placed,
        out_specs=(
            P("sp", None),
            P("sp", None),
            P("sp", None),
            P("sp", None),
            P("sp", None),
            P("sp", None),
        ),
        check_vma=False,
    )
```

profile of v0, /device:TPU:6, one launch (start us, length us, event | category | flops | bytes accessed | tf_op | source)
XLA Modules:
  0.0 249.4 jit_solution(16553010181526871349)
XLA Ops:
  7.2 1.4 copy.51
  8.5 1.1 copy.42
  9.7 9.4 %all-to-all-start = ((bf16[192,16,1,128]{3,0,2,1:T(8,128)(2,1)}), bf16[192,16,1,128]{3,0,2,1:T(8,128)(2,1)S(1)}, u32[]{:S(2)}, u32[]{:S(2)}) async-start(bf16[192,16,1,128]{3,0,2,1:T(8,128)(2,1)} %copy.42), calls=%async_computation | async-start | bytes 1572864 | tf_op jit(solution)/shard_map/all_to_all | solution.py:166
  19.2 1.1 copy.43
  20.3 10.3 %all-to-all-done = bf16[192,16,1,128]{3,0,2,1:T(8,128)(2,1)S(1)} async-done(((bf16[192,16,1,128]{3,0,2,1:T(8,128)(2,1)}), bf16[192,16,1,128]{3,0,2,1:T(8,128)(2,1)S(1)}, u32[]{:S(2)}, u32[]{:S(2)}) %all-to-all-start) | async-done | bytes 786464 | tf_op jit(solution)/shard_map/all_to_all | solution.py:166
  30.6 5.8 %all-to-all-start.1 = ((bf16[192,16,1,128]{3,0,2,1:T(8,128)(2,1)}), bf16[192,16,1,128]{3,0,2,1:T(8,128)(2,1)S(1)}, u32[]{:S(2)}, u32[]{:S(2)}) async-start(bf16[192,16,1,128]{3,0,2,1:T(8,128)(2,1)} %copy.43), calls=%async_computation.1 | async-start | bytes 1572864 | tf_op jit(solution)/shard_map/all_to_all | solution.py:167
  36.5 1.1 copy.44
  37.6 10.2 %all-to-all-done.1 = bf16[192,16,1,128]{3,0,2,1:T(8,128)(2,1)S(1)} async-done(((bf16[192,16,1,128]{3,0,2,1:T(8,128)(2,1)}), bf16[192,16,1,128]{3,0,2,1:T(8,128)(2,1)S(1)}, u32[]{:S(2)}, u32[]{:S(2)}) %all-to-all-start.1) | async-done | bytes 786464 | tf_op jit(solution)/shard_map/all_to_all | solution.py:167
  47.9 5.8 %all-to-all-start.2 = ((bf16[192,16,1,128]{3,0,2,1:T(8,128)(2,1)}), bf16[192,16,1,128]{3,0,2,1:T(8,128)(2,1)S(1)}, u32[]{:S(2)}, u32[]{:S(2)}) async-start(bf16[192,16,1,128]{3,0,2,1:T(8,128)(2,1)} %copy.44), calls=%async_computation.2 | async-start | bytes 1572864 | tf_op jit(solution)/shard_map/all_to_all | solution.py:168
  55.4 9.8 %all-to-all-done.2 = bf16[192,16,1,128]{3,0,2,1:T(8,128)(2,1)S(1)} async-done(((bf16[192,16,1,128]{3,0,2,1:T(8,128)(2,1)}), bf16[192,16,1,128]{3,0,2,1:T(8,128)(2,1)S(1)}, u32[]{:S(2)}, u32[]{:S(2)}) %all-to-all-start.2) | async-done | bytes 786464 | tf_op jit(solution)/shard_map/all_to_all | solution.py:168
  65.2 31.9 %while.10 = (s32[]{:T(128)}, bf16[6,1,512,128]{3,2,1,0:T(8,128)(2,1)S(1)}, s32[6,512]{1,0:T(8,128)S(1)}, s32[3072]{0:T(1024)S(1)}, bf16[6,1,512,128]{3,2,1,0:T(8...) while((s32[]{:T(128)}, ...), condition=%wide.region_5.6_spmd, body=%wide.region_2.5_spmd.sunk | while | flops 827456512 | bytes 20766816 | solution.py:158
  65.2 1.2 fusion.65
  66.4 1.9 fusion.66
  68.3 2.2 fusion.67
  70.5 1.2 fusion.65
  71.7 1.9 fusion.66
  73.6 2.2 fusion.67
  75.8 1.2 fusion.65
  77.0 1.9 fusion.66
  78.9 2.2 fusion.67
  81.1 1.2 fusion.65
  82.3 1.9 fusion.66
  84.2 2.2 fusion.67
  86.5 1.2 fusion.65
  87.7 1.9 fusion.66
  89.5 2.2 fusion.67
  91.8 1.2 fusion.65
  93.0 1.9 fusion.66
  94.8 2.2 fusion.67
  97.6 1.2 reduce.5
  98.8 1.1 reshape.153
  99.9 5.8 %all-to-all-start.3 = ((bf16[16,2,12288]{2,1,0:T(2,128)(2,1)}), bf16[16,2,12288]{2,1,0:T(2,128)(2,1)S(1)}, u32[]{:S(2)}, u32[]{:S(2)}) async-start(bf16[16,2,12288]{2,1,0:T(2,128)(2,1)} %reshape.153), calls=%async_computation.3 | async-start | bytes 1572864 | tf_op jit(solution)/shard_map/all_to_all | solution.py:171
  105.8 1.7 reshape.152
  107.9 1.2 reshape_reshape.12
  109.1 8.1 %all-to-all-done.3 = bf16[16,2,12288]{2,1,0:T(2,128)(2,1)S(1)} async-done(((bf16[16,2,12288]{2,1,0:T(2,128)(2,1)}), bf16[16,2,12288]{2,1,0:T(2,128)(2,1)S(1)}, u32[]{:S(2)}, u32[]{:S(2)}) %all-to-all-start.3) | async-done | bytes 786464 | tf_op jit(solution)/shard_map/all_to_all | solution.py:171
  117.2 0.7 reshape.154
  118.6 2.0 convolution_multiply_fusion
  120.6 1.4 reshape_reshape.15
  122.1 2.9 %convolution_multiply_fusion.1 = f32[2048,128]{1,0:T(8,128)S(1)} fusion(bf16[128,3072]{1,0:T(8,128)(2,1)} %reshape_reshape.12, bf16[1,192,3072]{2,1,0:T(8,128)(2,1)} %param.17, bf16[24,8,16,128]{3,2,1,0:T(8,128)(2,1)S(1)} %bitcast.105, bf16[192]{0:T(256)(128)(2,1)S(1)} %compare_convert_fusion), kind=kOutput, calls=%fused_computation.22 | convolution fusion | flops 252559360 | bytes 3801472 | tf_op jit(solution)/shard_map/dot_general | solution.py:109
  125.0 1.2 reshape_reshape.13
  126.2 1.9 pad_maximum_fusion
  128.0 1.7 reshape.149
  129.8 66.4 %reduce-scatter.2.cloned.1.call-done = f32[320,128]{1,0:T(8,128)} async-done(((f32[5120,128]{1,0:T(8,128)}), f32[320,128]{1,0:T(8,128)}) %reduce-scatter.2.cloned.1.call-update) | async-done | bytes 163856 | tf_op jit(solution)/shard_map/reduce_scatter | solution.py:47
  196.2 0.9 slice_bitcast_fusion
  197.1 0.8 slice_bitcast_fusion.1
  198.0 25.4 %all_to_all.75 = f32[32,1,1280]{2,1,0:T(1,128)S(1)} all-to-all(f32[32,1,1280]{2,1,0:T(1,128)S(1)} %bitcast.119), channel_id=1, replica_groups=mesh['rep'=32,'sp'=16] {'rep'}, dimensions={0} | all-to-all | bytes 327680 | tf_op jit(solution)/shard_map/all_to_all | solution.py:75
  223.5 17.5 %all_to_all.76 = f32[32,1,1280]{2,1,0:T(1,128)S(1)} all-to-all(f32[32,1,1280]{2,1,0:T(1,128)S(1)} %broadcast_in_dim.21), channel_id=1, replica_groups=mesh['rep'=32,'sp'=16] {'rep'}, dimensions={0} | all-to-all | bytes 327680 | tf_op jit(solution)/shard_map/all_to_all | solution.py:64
  241.1 0.7 multiply_add_fusion
  (55 shorter events, 3.9 us)
Async XLA Ops:
  7.2 11.9 %copy-start = (bf16[1,192,2048]{2,1,0:T(8,128)(2,1)S(1)}, bf16[1,192,2048]{2,1,0:T(8,128)(2,1)}, u32[]{:S(2)}) copy-start(bf16[1,192,2048]{2,1,0:T(8,128)(2,1)} %param.15) | copy-start | bytes 2359300
  9.7 26.7 %copy-start.1 = (bf16[1,192,2048]{2,1,0:T(8,128)(2,1)S(1)}, bf16[1,192,2048]{2,1,0:T(8,128)(2,1)}, u32[]{:S(2)}) copy-start(bf16[1,192,2048]{2,1,0:T(8,128)(2,1)} %param.16) | copy-start | bytes 2359300
  9.7 20.9 %all-to-all-start = ((bf16[192,16,1,128]{3,0,2,1:T(8,128)(2,1)}), bf16[192,16,1,128]{3,0,2,1:T(8,128)(2,1)S(1)}, u32[]{:S(2)}, u32[]{:S(2)}) async-start(bf16[192,16,1,128]{3,0,2,1:T(8,128)(2,1)} %copy.42), calls=%async_computation | async-start | bytes 1572864 | tf_op jit(solution)/shard_map/all_to_all | solution.py:166
  20.3 33.4 %copy-start.2 = (f32[8,3072]{1,0:T(8,128)S(1)}, f32[8,3072]{1,0:T(8,128)}, u32[]{:S(2)}) copy-start(f32[8,3072]{1,0:T(8,128)} %param.21) | copy-start | bytes 294916
  20.3 33.5 %copy-start.3 = (f32[128,128]{1,0:T(8,128)S(1)}, f32[128,128]{1,0:T(8,128)}, u32[]{:S(2)}) copy-start(f32[128,128]{1,0:T(8,128)} %param.20) | copy-start | bytes 196612
  20.3 34.8 %copy-start.9 = (s32[1,3]{1,0:T(1,128)S(1)}, s32[1,3]{1,0:T(1,128)}, u32[]{:S(2)}) copy-start(s32[1,3]{1,0:T(1,128)} %param.19) | copy-start | bytes 40
  30.6 17.3 %all-to-all-start.1 = ((bf16[192,16,1,128]{3,0,2,1:T(8,128)(2,1)}), bf16[192,16,1,128]{3,0,2,1:T(8,128)(2,1)S(1)}, u32[]{:S(2)}, u32[]{:S(2)}) async-start(bf16[192,16,1,128]{3,0,2,1:T(8,128)(2,1)} %copy.43), calls=%async_computation.1 | async-start | bytes 1572864 | tf_op jit(solution)/shard_map/all_to_all | solution.py:167
  47.9 17.3 %all-to-all-start.2 = ((bf16[192,16,1,128]{3,0,2,1:T(8,128)(2,1)}), bf16[192,16,1,128]{3,0,2,1:T(8,128)(2,1)S(1)}, u32[]{:S(2)}, u32[]{:S(2)}) async-start(bf16[192,16,1,128]{3,0,2,1:T(8,128)(2,1)} %copy.44), calls=%async_computation.2 | async-start | bytes 1572864 | tf_op jit(solution)/shard_map/all_to_all | solution.py:168
  53.7 52.1 %all-gather.3.cloned.1.call-start = ((), (), s32[]{:S(2)}) async-start(), calls=%async_computation.8 | async-start | bytes 1392640 | tf_op jit(solution)/shard_map/all_gather | solution.py:27
  99.9 17.3 %all-to-all-start.3 = ((bf16[16,2,12288]{2,1,0:T(2,128)(2,1)}), bf16[16,2,12288]{2,1,0:T(2,128)(2,1)S(1)}, u32[]{:S(2)}, u32[]{:S(2)}) async-start(bf16[16,2,12288]{2,1,0:T(2,128)(2,1)} %reshape.153), calls=%async_computation.3 | async-start | bytes 1572864 | tf_op jit(solution)/shard_map/all_to_all | solution.py:171
  105.7 90.5 %reduce-scatter.2.cloned.1.call-start = ((), (), s32[]{:S(2)}) async-start(), calls=%async_computation.7 | async-start | bytes 2785280 | tf_op jit(solution)/shard_map/reduce_scatter | solution.py:47
  129.8 111.3 %copy-start.5 = (f32[8,3072]{1,0:T(8,128)S(1)}, f32[8,3072]{1,0:T(8,128)}, u32[]{:S(2)}) copy-start(f32[8,3072]{1,0:T(8,128)} %param.25) | copy-start | bytes 294916
  129.8 111.3 %copy-start.6 = (f32[8,3072]{1,0:T(8,128)S(1)}, f32[8,3072]{1,0:T(8,128)}, u32[]{:S(2)}) copy-start(f32[8,3072]{1,0:T(8,128)} %param.24) | copy-start | bytes 294916
  129.8 112.0 %copy-start.4 = (f32[128,128]{1,0:T(8,128)S(1)}, f32[128,128]{1,0:T(8,128)}, u32[]{:S(2)}) copy-start(f32[128,128]{1,0:T(8,128)} %param.20) | copy-start | bytes 196612
  129.8 112.0 %copy-start.7 = (f32[128,128]{1,0:T(8,128)S(1)}, f32[128,128]{1,0:T(8,128)}, u32[]{:S(2)}) copy-start(f32[128,128]{1,0:T(8,128)} %param.23) | copy-start | bytes 196612
  129.8 112.0 %copy-start.8 = (f32[128,128]{1,0:T(8,128)S(1)}, f32[128,128]{1,0:T(8,128)}, u32[]{:S(2)}) copy-start(f32[128,128]{1,0:T(8,128)} %param.22) | copy-start | bytes 196612
Sparse Core Ops, SparseCore 0:
  57.2 37.2 all-gather.2
  130.0 66.1 reduce-scatter.1
where the time goes:
time: 251 us; the launch traced here: 249 us
  waiting for transfers between devices  105 us (42%)
  blocking collectives  42.9 us (17%)
  starting transfers between devices  26.8 us (11%)
  matrix products  25.5 us (10%)
  local copies, waits for them, and re-layouts  17.5 us (7%)
  other arithmetic  16.8 us (7%)
  between operations  14.9 us (6%)
    reduce_scatter x1, waiting for transfers between devices, sum_packed(): lax.psum_scatter(lines, axis, tiled=True).reshape(-1)  66.4 us
    all_to_all x1, blocking collectives, summed_on_arrival(): lax.all_to_all(blocks, axis, split_axis=0, concat_axis=0, tiled=True)  25.4 us
    all_to_all x1, blocking collectives, sent_to_all(): lax.all_to_all(jnp.broadcast_to(array[None], (peers, *array.shape)), axis...  17.5 us
    dot_general x6, matrix products, one_block(): jnp.dot(weights, value_head, preferred_element_type=jnp.float32) / row_total  13.4 us
    reduce_sum x6, other arithmetic, one_block(): row_total = jnp.sum(exponent, axis=1, keepdims=True)  11.1 us
    all_to_all x1, waiting for transfers between devices, per_device(): lax.all_to_all(query_split, 'sp', split_axis=1, concat_axis=0, tiled=True)  10.3 us
    all_to_all x1, waiting for transfers between devices, per_device(): lax.all_to_all(key_split, 'sp', split_axis=1, concat_axis=0, tiled=True)  10.2 us
    all_to_all x1, waiting for transfers between devices, per_device(): lax.all_to_all(value_split, 'sp', split_axis=1, concat_axis=0, tiled=True)  9.78 us
  transfers between devices with their start and end apart: 6, of which 5 were waited for; matrix products, arithmetic and copies ran while one was open for 17% of the time, Pallas kernels for 0%

commit v1 on v0

v1 whole, which is shorter than its diff:
```python
import functools
import math

import jax
import jax.numpy as jnp
from jax import lax
from jax.experimental import pallas as pl
from jax.experimental.pallas import tpu as pltpu
from jax.sharding import PartitionSpec as P

HD = 128
MAX_CLIPS = 3
MESH = pl.DeviceIdType.MESH

first_rate = 0.9
second_rate = 0.999
adam_steps = 100.0
adam_epsilon = 1e-08
decay_rate = 0.1

EXP2_SCALE = HD ** (-0.5) * math.log2(math.e)
MASK = -131072.0
KEY_CHUNKS = 4


def adamw(param, grad, moment, square):
    momentum = first_rate * moment + (1.0 - first_rate) * grad
    variance = second_rate * square + (1.0 - second_rate) * grad * grad
    first_hat = momentum / (1.0 - first_rate**adam_steps)
    second_hat = variance / (1.0 - second_rate**adam_steps)
    update = first_hat / (jnp.sqrt(second_hat) + adam_epsilon) + decay_rate * param
    return (momentum, variance, update)


def remote(src, dst, send_sem, recv_sem, device):
    return pltpu.make_async_remote_copy(
        src_ref=src,
        dst_ref=dst,
        send_sem=send_sem,
        recv_sem=recv_sem,
        device_id=device,
        device_id_type=MESH,
    )


def each(n, body, start=0):
    def step(i, carry):
        body(i)
        return carry

    lax.fori_loop(start, n, step, 0)


def step_kernel(
    dims,
    count_ref,
    lengths_ref,
    q_hbm,
    k_hbm,
    v_hbm,
    og_hbm,
    ain_hbm,
    aout_hbm,
    gin_ref,
    gout_ref,
    q_all,
    k_all,
    v_all,
    scores_buf,
    high_buf,
    mixed,
    attended,
    og_all,
    ain_own,
    aout_own,
    ain_cast,
    aout_cast,
    ain_all,
    aout_all,
    slopes_all,
    adapted_all,
    summed,
    chip_in,
    in_bufs,
    out_bufs,
    load_sems,
    og_s,
    og_r,
    ad_s,
    ad_r,
    k_s,
    k_r,
    v_s,
    v_r,
    q_s,
    q_r,
    o_s,
    o_r,
    ai_s,
    ai_r,
    ao_s,
    ao_r,
    sl_s,
    sl_r,
    chip_s,
    chip_r,
    az_s,
    az_r,
    cz_s,
    cz_r,
    half_s,
    half_r,
    in_sems,
    out_sems,
):
    tok, groups, nz, ny = dims
    chips = groups // 2
    tokens = tok * groups
    rank = ain_hbm.shape[1]
    inner = HD * groups
    me = lax.axis_index("sp")
    rep = lax.axis_index("rep")
    chip = me // 2
    core = lax.rem(me, 2)
    partner = me + 1 - 2 * core
    z = rep // ny
    y = lax.rem(rep, ny)

    def rows(s):
        return pl.ds(pl.multiple_of(s * tok, tok), tok)

    def lanes(s):
        return pl.ds(pl.multiple_of(s * HD, HD), HD)

    def same_core(i):
        return 2 * lax.rem(chip + i, chips) + core

    barrier = pltpu.get_barrier_semaphore()

    def greet_sp(i):
        pl.semaphore_signal(
            barrier, inc=1, device_id={"sp": lax.rem(me + i, groups)}, device_id_type=MESH
        )

    def greet_z(i):
        pl.semaphore_signal(
            barrier,
            inc=1,
            device_id={"rep": lax.rem(z + i, nz) * ny + y},
            device_id_type=MESH,
        )

    def greet_y(i):
        pl.semaphore_signal(
            barrier,
            inc=1,
            device_id={"rep": z * ny + lax.rem(y + i, ny)},
            device_id_type=MESH,
        )

    each(groups, greet_sp, 1)
    each(nz, greet_z, 1)
    each(ny, greet_y, 1)

    load_og = pltpu.make_async_copy(og_hbm.at[0], og_all.at[core], load_sems.at[0])
    load_ain = pltpu.make_async_copy(ain_hbm, ain_own, load_sems.at[1])
    load_aout = pltpu.make_async_copy(aout_hbm, aout_own, load_sems.at[2])
    load_ain.start()
    load_aout.start()
    load_og.start()
    ends = []
    for j in range(MAX_CLIPS):
        length = jnp.where(count_ref[0] > j, lengths_ref[0, j], 0)
        ends.append(length if j == 0 else ends[-1] + length)

    def segment(positions):
        return sum((positions >= e).astype(jnp.int32) for e in ends)

    block = 2 * tok

    def features(b):
        r = pl.ds(pl.multiple_of(b * block, block), block)
        at = b * block + lax.broadcasted_iota(jnp.int32, (block, HD), 0)
        feature = lax.broadcasted_iota(jnp.int32, (block, HD), 1)
        seg = segment(at)
        same = seg == feature
        k_all[r, HD:] = jnp.where(same, 1.0, 0.0).astype(jnp.bfloat16)
        other = jnp.where(feature <= MAX_CLIPS, MASK, 0.0)
        q_all[r, HD:] = jnp.where(same, 0.0, other).astype(jnp.bfloat16)

    each(chips, features)
    mine = me * tok + lax.broadcasted_iota(jnp.int32, (tok, rank), 0)
    live = segment(mine) < MAX_CLIPS
    load_ain.wait()
    load_aout.wait()
    ain_cast[...] = ain_own[...].astype(jnp.bfloat16)
    aout_cast[...] = aout_own[...].astype(jnp.bfloat16)
    pl.semaphore_wait(barrier, groups + nz + ny - 3)

    half = groups // 2
    in_rows = HD // nz
    out_cols = gout_ref.shape[1] // nz
    side = me // half
    z_cols = pl.ds(pl.multiple_of(z * out_cols, out_cols), out_cols)
    z_rows = pl.ds(pl.multiple_of(z * in_rows, in_rows), in_rows)

    def share_device(i):
        return 2 * lax.rem(chip + i, chips) + side

    def aout_share(device):
        return remote(
            aout_cast.at[:, z_cols],
            aout_all.at[me, :, z_cols],
            ao_s.at[device],
            ao_r.at[me],
            {"sp": device},
        )

    def ain_share(device):
        return remote(
            ain_cast.at[z_rows], ain_all.at[me, z_rows], ai_s.at[device], ai_r.at[me], {"sp": device}
        )

    @pl.when(core == side)
    def _():
        pltpu.make_async_copy(
            aout_cast.at[:, z_cols], aout_all.at[me, :, z_cols], ao_r.at[me]
        ).start()
        pltpu.make_async_copy(ain_cast.at[z_rows], ain_all.at[me, z_rows], ai_r.at[me]).start()

    @pl.when(core != side)
    def _():
        aout_share(partner).start()
        ain_share(partner).start()

    def send_share(i):
        aout_share(share_device(i)).start()
        ain_share(share_device(i)).start()

    each(chips, send_share, 1)

    def head_to(src, dst, s, r, device):
        return remote(
            src.at[0, :, lanes(device)],
            dst.at[rows(me), pl.ds(0, HD)],
            s.at[device],
            r.at[me],
            {"sp": device},
        )

    def own_head(src, dst, r):
        return pltpu.make_async_copy(
            src.at[0, :, lanes(me)], dst.at[rows(me), pl.ds(0, HD)], r.at[me]
        )

    def to_peer(i):
        return lax.rem(me - i + groups, groups)

    own_head(k_hbm, k_all, k_r).start()
    each(groups, lambda i: head_to(k_hbm, k_all, k_s, k_r, to_peer(i)).start(), 1)
    own_head(v_hbm, v_all, v_r).start()
    each(groups, lambda i: head_to(v_hbm, v_all, v_s, v_r, to_peer(i)).start(), 1)
    own_head(q_hbm, q_all, q_r).start()
    each(groups, lambda i: head_to(q_hbm, q_all, q_s, q_r, to_peer(i)).start(), 1)

    send_og = remote(og_hbm.at[0], og_all.at[core], og_s, og_r, {"sp": partner})
    send_og.start()

    owners = pl.ds(pl.multiple_of(core * half, half), half)

    def wait_share(i):
        owner = core * half + i
        remote(
            aout_cast.at[:, z_cols],
            aout_all.at[owner, :, z_cols],
            ao_s.at[owner],
            ao_r.at[owner],
            {"sp": partner},
        ).wait_recv()
        remote(
            ain_cast.at[z_rows],
            ain_all.at[owner, z_rows],
            ai_s.at[owner],
            ai_r.at[owner],
            {"sp": partner},
        ).wait_recv()

    each(half, wait_share)

    def z_peer(i):
        return lax.rem(z + i, nz)

    def aout_along(p, origin):
        cols = pl.ds(pl.multiple_of(origin * out_cols, out_cols), out_cols)
        part = aout_all.at[owners, :, cols]
        return remote(part, part, az_s.at[p], az_r.at[origin], {"rep": p * ny + y})

    def ain_along(p, origin):
        lines = pl.ds(pl.multiple_of(origin * in_rows, in_rows), in_rows)
        part = ain_all.at[owners, lines]
        return remote(part, part, cz_s.at[p], cz_r.at[origin], {"rep": p * ny + y})

    def send_along(i):
        aout_along(z_peer(i), z).start()
        ain_along(z_peer(i), z).start()

    each(nz, send_along, 1)

    def wait_along(i):
        aout_along(z_peer(i), z_peer(i)).wait_recv()
        ain_along(z_peer(i), z_peer(i)).wait_recv()

    each(nz, wait_along, 1)
    swap_out = remote(
        aout_all.at[owners], aout_all.at[owners], half_s.at[0], half_r.at[0], {"sp": partner}
    )
    swap_in = remote(
        ain_all.at[owners], ain_all.at[owners], half_s.at[1], half_r.at[1], {"sp": partner}
    )
    swap_out.start()
    swap_in.start()
    swap_out.wait_recv()
    swap_in.wait_recv()
    load_og.wait()

    outer = jnp.concatenate([aout_all[i].astype(jnp.float32) for i in range(groups)], axis=0)
    slopes = lax.dot_general(
        og_all[core],
        outer.astype(jnp.bfloat16),
        (((1,), (1,)), ((), ())),
        preferred_element_type=jnp.float32,
    ) * rank ** (-0.5)
    slopes_all[rows(me)] = jnp.where(live, slopes, 0.0).astype(jnp.bfloat16)

    def slopes_to(owner, device, slot):
        return remote(
            slopes_all.at[rows(owner)],
            slopes_all.at[rows(owner)],
            sl_s.at[slot],
            sl_r.at[owner],
            {"sp": device},
        )

    slopes_to(me, partner, 0).start()
    each(chips, lambda i: slopes_to(me, same_core(i), i).start(), 1)

    def wait_head(dst, r, s, peer):
        remote(
            dst.at[rows(peer), pl.ds(0, HD)],
            dst.at[rows(peer), pl.ds(0, HD)],
            s.at[peer],
            r.at[peer],
            {"sp": partner},
        ).wait_recv()

    each(groups, lambda i: wait_head(k_all, k_r, k_s, i))
    each(groups, lambda i: wait_head(v_all, v_r, v_s, i))

    def chip_of(i):
        return lax.rem(chip + i, chips)

    def block_rows(i):
        return pl.ds(pl.multiple_of(chip_of(i) * block, block), block)

    def wait_queries(i):
        wait_head(q_all, q_r, q_s, 2 * chip_of(i))
        wait_head(q_all, q_r, q_s, 2 * chip_of(i) + 1)

    width = tokens // KEY_CHUNKS

    def scores(i, slot):
        query = q_all[block_rows(i), :]
        high = None
        for c in range(KEY_CHUNKS):
            s = lax.dot_general(
                query,
                k_all[c * width : (c + 1) * width, :],
                (((1,), (1,)), ((), ())),
                preferred_element_type=jnp.float32,
            )
            scores_buf[slot, :, c * width : (c + 1) * width] = s
            for j in range(width // HD):
                piece = s[:, j * HD : (j + 1) * HD]
                high = piece if high is None else jnp.maximum(high, piece)
        high_buf[slot] = jnp.broadcast_to(jnp.max(high, axis=1, keepdims=True), (block, HD))

    def finish(i, slot):
        high = high_buf[slot][:, :1]
        total = None
        row_total = None
        for c in range(KEY_CHUNKS):
            s = scores_buf[slot, :, c * width : (c + 1) * width]
            exponent = jnp.exp2((s - high) * EXP2_SCALE)
            for j in range(width // HD):
                piece = exponent[:, j * HD : (j + 1) * HD]
                row_total = piece if row_total is None else row_total + piece
            term = jnp.dot(
                exponent.astype(jnp.bfloat16),
                v_all[c * width : (c + 1) * width, :],
                preferred_element_type=jnp.float32,
            )
            total = term if total is None else total + term
        row_total = jnp.sum(row_total, axis=1, keepdims=True)
        mixed[block_rows(i), :] = (total / row_total).astype(jnp.bfloat16)

    def mixed_to(device):
        return remote(
            mixed.at[rows(device)],
            attended.at[:, lanes(me)],
            o_s.at[device],
            o_r.at[me],
            {"sp": device},
        )

    def own_mixed():
        return pltpu.make_async_copy(mixed.at[rows(me)], attended.at[:, lanes(me)], o_r.at[me])

    def give_back(i):
        for c in range(2):
            device = 2 * chip_of(i) + c

            @pl.when(device == me)
            def _():
                own_mixed().start()

            @pl.when(device != me)
            def _():
                mixed_to(device).start()

    wait_queries(0)
    scores(0, 0)

    def two_blocks(t):
        i = 2 * t
        wait_queries(i + 1)
        scores(i + 1, 1)
        finish(i, 0)
        give_back(i)
        wait_queries(i + 2)
        scores(i + 2, 0)
        finish(i + 1, 1)
        give_back(i + 1)

    each(chips // 2 - 1, two_blocks)

    def forward_slopes(i):
        owner = same_core(i)
        slopes_to(owner, partner, chips + i).wait_recv()
        slopes_to(owner, partner, chips + i).start()

    each(chips, forward_slopes, 1)

    wait_queries(chips - 1)
    scores(chips - 1, 1)
    finish(chips - 2, 0)
    give_back(chips - 2)
    finish(chips - 1, 1)
    give_back(chips - 1)

    each(chips, lambda i: slopes_to(2 * i + 1 - core, partner, 0).wait_recv())
    grad_in = lax.dot_general(
        mixed[...], slopes_all[...], (((0,), (0,)), ((), ())), preferred_element_type=jnp.float32
    ) * inner ** (-0.5)
    out_tiles = out_cols // HD

    def y_peer(i):
        return lax.rem(y + i, ny)

    class Replicas:
        def __init__(self, bufs, sems):
            self.pack, self.z_in, self.y_out, self.y_in, self.z_out, self.whole = bufs
            self.zi_s, self.zi_r, self.y_s, self.y_r, self.zo_s, self.zo_r = sems

        def z_copy(self, p, origin):
            return remote(
                self.pack.at[p],
                self.z_in.at[origin],
                self.zi_s.at[p],
                self.zi_r.at[origin],
                {"rep": p * ny + y},
            )

        def y_copy(self, p, origin):
            return remote(
                self.y_out,
                self.y_in.at[origin],
                self.y_s.at[p],
                self.y_r.at[origin],
                {"rep": z * ny + p},
            )

        def back_copy(self, p, origin):
            return remote(
                self.z_out,
                self.whole.at[origin],
                self.zo_s.at[p],
                self.zo_r.at[origin],
                {"rep": p * ny + y},
            )

        def start(self):
            each(nz, lambda i: self.z_copy(z_peer(i), z).start(), 1)
            self.z_in[z] = self.pack[z]

        def across(self):
            each(nz, lambda i: self.z_copy(z_peer(i), z_peer(i)).wait_recv(), 1)
            total = self.z_in[0]
            for p in range(1, nz):
                total = total + self.z_in[p]
            self.y_out[...] = total
            each(ny, lambda i: self.y_copy(y_peer(i), y).start(), 1)
            self.y_in[y] = total

        def back(self):
            each(ny, lambda i: self.y_copy(y_peer(i), y_peer(i)).wait_recv(), 1)
            total = self.y_in[0]
            for p in range(1, ny):
                total = total + self.y_in[p]
            self.z_out[...] = total
            each(nz, lambda i: self.back_copy(z_peer(i), z).start(), 1)
            self.whole[z] = total

        def arrive(self):
            each(nz, lambda i: self.back_copy(z_peer(i), z_peer(i)).wait_recv(), 1)

        def sent(self):
            each(nz, lambda i: self.z_copy(z_peer(i), z).wait_send(), 1)
            each(ny, lambda i: self.y_copy(y_peer(i), y).wait_send(), 1)
            each(nz, lambda i: self.back_copy(z_peer(i), z).wait_send(), 1)

    sum_in = Replicas(in_bufs, in_sems)
    sum_out = Replicas(out_bufs, out_sems)
    for p in range(nz):
        sum_in.pack[p] = grad_in[p * in_rows : (p + 1) * in_rows]
    sum_in.start()

    def wait_mixed(i):
        remote(
            mixed.at[rows(i)], attended.at[:, lanes(i)], o_s.at[i], o_r.at[i], {"sp": partner}
        ).wait_recv()

    each(groups, wait_mixed)
    adapted = jnp.dot(
        attended[...], ain_all[...].reshape(inner, rank), preferred_element_type=jnp.float32
    )
    adapted_all[core] = jnp.where(live, adapted * inner ** (-0.5), 0.0).astype(jnp.bfloat16)
    send_adapted = remote(adapted_all.at[core], adapted_all.at[core], ad_s, ad_r, {"sp": partner})
    send_adapted.start()
    sum_in.across()
    send_og.wait_recv()
    send_adapted.wait_recv()
    term_out = lax.dot_general(
        adapted_all[...].reshape(block, rank),
        og_all[...].reshape(block, og_all.shape[2]),
        (((0,), (0,)), ((), ())),
        preferred_element_type=jnp.float32,
    ) * rank ** (-0.5)
    depth = rank // groups

    for j in range(chips):
        at = 2 * j * depth
        summed[j] = jnp.where(
            core == 0, term_out[at : at + depth], term_out[at + depth : at + 2 * depth]
        )

    def chunk_to(i):
        j = lax.rem(chip + i, chips)
        return remote(
            summed.at[j], chip_in.at[chip], chip_s.at[j], chip_r.at[chip], {"sp": 2 * j + core}
        )

    each(chips, lambda i: chunk_to(i).start(), 1)
    chip_in[chip] = summed[chip]

    def wait_chunk(i):
        j = lax.rem(chip + i, chips)
        remote(
            summed.at[j], chip_in.at[j], chip_s.at[j], chip_r.at[j], {"sp": 2 * j + core}
        ).wait_recv()

    sum_in.back()
    each(chips, wait_chunk, 1)
    grad_out = chip_in[0]
    for j in range(1, chips):
        grad_out = grad_out + chip_in[j]

    for p in range(nz):
        for t in range(out_tiles):
            at = p * out_cols + t * HD
            sum_out.pack[p, t * 8 : (t + 1) * 8] = grad_out[:, at : at + HD]
    sum_out.start()
    sum_in.arrive()
    for p in range(nz):
        gin_ref[p * in_rows : (p + 1) * in_rows] = sum_in.whole[p]
    sum_out.across()


    @pl.when(core != side)
    def _():
        aout_share(partner).wait_send()
        ain_share(partner).wait_send()

    def sent_to_chips(i):
        aout_share(share_device(i)).wait_send()
        ain_share(share_device(i)).wait_send()
        slopes_to(me, same_core(i), i).wait_send()
        slopes_to(same_core(i), partner, chips + i).wait_send()
        chunk_to(i).wait_send()

    each(chips, sent_to_chips, 1)
    slopes_to(me, partner, 0).wait_send()
    send_og.wait_send()
    send_adapted.wait_send()
    swap_out.wait_send()
    swap_in.wait_send()

    def sent_along(i):
        aout_along(z_peer(i), z).wait_send()
        ain_along(z_peer(i), z).wait_send()

    each(nz, sent_along, 1)

    def sent_to_group(i):
        peer = to_peer(i)
        head_to(k_hbm, k_all, k_s, k_r, peer).wait_send()
        head_to(v_hbm, v_all, v_s, v_r, peer).wait_send()
        head_to(q_hbm, q_all, q_s, q_r, peer).wait_send()
        mixed_to(peer).wait_send()

    each(groups, sent_to_group, 1)
    sum_out.back()
    sum_in.sent()
    sum_out.sent()
    sum_out.arrive()
    for p in range(nz):
        for t in range(out_tiles):
            at = p * out_cols + t * HD
            gout_ref[:, at : at + HD] = sum_out.whole[p, t * 8 : (t + 1) * 8]


def adamw_kernel(*refs):
    ins, outs = refs[:8], refs[8:]
    for at in range(2):
        param, grad, moment, square = (r[...] for r in ins[4 * at : 4 * at + 4])
        for ref, value in zip(outs[3 * at : 3 * at + 3], adamw(param, grad, moment, square)):
            ref[...] = value


def per_device(
    queries,
    key_rows,
    values,
    out_grad,
    clip_count,
    clip_lengths,
    adapter_in,
    adapter_out,
    moment_in,
    square_in,
    moment_out,
    square_out,
):
    tok = queries.shape[1]
    width = out_grad.shape[2]
    rank = adapter_in.shape[1]
    groups = lax.axis_size("sp")
    chips = groups // 2
    reps = lax.axis_size("rep")
    ny = 4 if reps % 4 == 0 and reps > 4 else 1
    nz = reps // ny
    tokens = tok * groups
    depth = rank // groups
    in_lines, out_lines = HD // nz, (width // nz // HD) * 8
    bf16, f32 = jnp.bfloat16, jnp.float32
    vmem = pl.BlockSpec(memory_space=pltpu.VMEM)
    smem = pl.BlockSpec(memory_space=pltpu.SMEM)
    hbm = pl.BlockSpec(memory_space=pl.ANY)
    dma = pltpu.SemaphoreType.DMA

    def sum_bufs(lines):
        return [
            pltpu.VMEM((nz, lines, HD), f32),
            pltpu.VMEM((nz, lines, HD), f32),
            pltpu.VMEM((lines, HD), f32),
            pltpu.VMEM((ny, lines, HD), f32),
            pltpu.VMEM((lines, HD), f32),
            pltpu.VMEM((nz, lines, HD), f32),
        ]

    sum_sems = [dma((n,)) for n in (nz, nz, ny, ny, nz, nz)]
    grad_in, grad_out = pl.pallas_call(
        functools.partial(step_kernel, (tok, groups, nz, ny)),
        name="adapter_step",
        out_shape=(
            jax.ShapeDtypeStruct((HD, rank), f32),
            jax.ShapeDtypeStruct((depth, width), f32),
        ),
        in_specs=[smem, smem, hbm, hbm, hbm, hbm, hbm, hbm],
        out_specs=(vmem, vmem),
        scratch_shapes=[
            pltpu.VMEM((tokens, 2 * HD), bf16),
            pltpu.VMEM((tokens, 2 * HD), bf16),
            pltpu.VMEM((tokens, HD), bf16),
            pltpu.VMEM((2, 2 * tok, tokens), f32),
            pltpu.VMEM((2, 2 * tok, HD), f32),
            pltpu.VMEM((tokens, HD), bf16),
            pltpu.VMEM((tok, groups * HD), bf16),
            pltpu.VMEM((2, tok, width), bf16),
            pltpu.VMEM((HD, rank), f32),
            pltpu.VMEM((depth, width), f32),
            pltpu.VMEM((HD, rank), bf16),
            pltpu.VMEM((depth, width), bf16),
            pltpu.VMEM((groups, HD, rank), bf16),
            pltpu.VMEM((groups, depth, width), bf16),
            pltpu.VMEM((tokens, rank), bf16),
            pltpu.VMEM((2, tok, rank), bf16),
            pltpu.VMEM((chips, depth, width), f32),
            pltpu.VMEM((chips, depth, width), f32),
            sum_bufs(in_lines),
            sum_bufs(out_lines),
            dma((3,)),
        ]
        + [dma(())] * 4
        + [dma((groups,))] * 14
        + [dma((chips,))] * 2
        + [dma((nz,))] * 4
        + [dma((2,))] * 2
        + [sum_sems, sum_sems],
        compiler_params=pltpu.CompilerParams(
            collective_id=0, has_side_effects=True, vmem_limit_bytes=60 * 2**20
        ),
    )(
        clip_count,
        clip_lengths,
        queries,
        key_rows,
        values,
        out_grad,
        adapter_in,
        adapter_out,
    )
    return tuple(
        pl.pallas_call(
            adamw_kernel,
            name="adamw",
            out_shape=[jax.ShapeDtypeStruct(a.shape, f32) for a in [grad_in] * 3 + [grad_out] * 3],
            in_specs=[vmem] * 8,
            out_specs=[vmem] * 6,
        )(
            adapter_in,
            grad_in,
            moment_in,
            square_in,
            adapter_out,
            grad_out,
            moment_out,
            square_out,
        )
    )


def solution(mesh):
    placed = (
        P("rep", "sp", None),
        P("rep", "sp", None),
        P("rep", "sp", None),
        P("rep", "sp", None),
        P("rep"),
        P("rep", None),
        P("sp", None),
        P("sp", None),
        P("sp", None),
        P("sp", None),
        P("sp", None),
        P("sp", None),
    )
    return jax.shard_map(
        per_device,
        mesh=mesh,
        in_specs=placed,
        out_specs=(
            P("sp", None),
            P("sp", None),
            P("sp", None),
            P("sp", None),
            P("sp", None),
            P("sp", None),
        ),
        check_vma=False,
    )
```

time: 251 us -> 99.6 us (0.40)
  waiting for transfers between devices: 105 us -> 0 us
  Pallas kernels: 0 us -> 98.1 us
  blocking collectives: 42.9 us -> 0 us
  starting transfers between devices: 26.8 us -> 0 us
  matrix products: 25.5 us -> 0 us
  local copies, waits for them, and re-layouts: 17.5 us -> 0 us
  other arithmetic: 16.8 us -> 0 us
  between operations: 14.9 us -> 1.29 us
    pallas_call x0 -> x2, Pallas kernels: none -> 98.1 us  [the longest x1 96.1 us: per_device(): pl.pallas_call(functools.partial(step_kernel, (tok, groups, nz, ny)), nam...]
    reduce_scatter x1 -> x0, waiting for transfers between devices: 66.4 us -> none  [sum_packed(): lax.psum_scatter(lines, axis, tiled=True).reshape(-1)]
    all_to_all x2 -> x0, blocking collectives: 42.9 us -> none  [the longest x1 25.4 us: summed_on_arrival(): lax.all_to_all(blocks, axis, split_axis=0, concat_axis=0, tiled=True)]
    all_to_all x4 -> x0, waiting for transfers between devices: 38.4 us -> none  [the longest x1 10.3 us: per_device(): lax.all_to_all(query_split, 'sp', split_axis=1, concat_axis=0, tiled=True)]
    all_to_all x4 -> x0, starting transfers between devices: 26.7 us -> none  [the longest x1 9.39 us: per_device(): lax.all_to_all(query_split, 'sp', split_axis=1, concat_axis=0, tiled=True)]
    dot_general x14 -> x0, matrix products: 25.5 us -> none  [the longest x6 13.4 us: one_block(): jnp.dot(weights, value_head, preferred_element_type=jnp.float32) / row_total]
    reduce_sum x8 -> x0, other arithmetic: 11.3 us -> none  [the longest x6 11.1 us: one_block(): row_total = jnp.sum(exponent, axis=1, keepdims=True)]
    reshape x6 -> x0, local copies, waits for them, and re-layouts: 5.07 us -> none  [the longest x1 1.73 us: sum_packed(): jnp.pad(lines, ((0, 0), (0, extent * 128 - lines.shape[1])))]
  transfers between devices with their start and end apart: 6 -> 0, of which waited for: 5 -> 0; matrix products, arithmetic and copies ran while one was open for 17% -> 0% of each run, Pallas kernels for 0% -> 0%
where the time goes in v1:
time: 99.6 us; the launch traced here: 99.4 us
  Pallas kernels  98.1 us (98%)
  between operations  1.29 us (1%)
    pallas_call x1, Pallas kernels, per_device(): pl.pallas_call(functools.partial(step_kernel, (tok, groups, nz, ny)), nam...  96.1 us

profile of v1, /device:TPU:6, one launch (start us, length us, event | category | flops | bytes accessed | tf_op | source)
XLA Modules:
  0.0 99.4 jit_solution(8871130587801135804)
XLA Ops:
  1.3 96.1 %adapter_step.1 = (f32[128,128]{1,0:T(8,128)}, f32[8,3072]{1,0:T(8,128)}) custom-call(s32[1]{0:T(128)S(6)} %copy.18.count_ref, s32[1,3]{1,0:T(1,128)} %lengths_ref.1, bf16[1,192,2048]{2,1,0:T(8,128)(2,1)} %q_hbm.1, bf16[1,192,2048]{2,1,0:T(8,128)(2,1)} %k_hbm.1, bf16[1,192,2048]{2,1,0:T(8,128)(2,1)} %v_hbm.1, bf16[1,192,3072]{2,1,0:T(8,128)(2,1)} %og_hbm.1, ...), custom_call_target="tpu_custom_call" | custom-call | tf_op jit(solution)/shard_map/adapter_step/pallas_call | solution.py:691
  97.4 2.0 %adamw.1 = (f32[128,128]{1,0:T(8,128)}, f32[128,128]{1,0:T(8,128)}, f32[128,128]{1,0:T(8,128)}, f32[8,3072]{1,0:T(8,128)}, f32[8,3072]{1,0:T(8,128)}, /*index=5*/f32[8,3072]{1,0:T(8,128)}) custom-call(f32[128,128]{1,0:T(8,128)} %refs_0_.1, f32[128,128]{1,0:T(8,128)} %get-tuple-element.8.refs_1_, f32[128,128]{1,0:T(8,128)} %refs_2_.1, f32[128,128]{1,0:T(8,128)} %refs_3_.1, ...), custom_call_target="tpu_custom_call" | custom-call | tf_op jit(solution)/shard_map/adamw/pallas_call | solution.py:743

commit v2 on v1

--- a/solution.py
+++ b/solution.py
@@ -81,6 +81,10 @@
     adapted_all,
     summed,
     chip_in,
+    z_first,
+    z_first_in,
+    tiles,
+    tile_in,
     in_bufs,
     out_bufs,
     load_sems,
@@ -104,6 +108,10 @@
     sl_r,
     chip_s,
     chip_r,
+    ti_s,
+    ti_r,
+    zf_s,
+    zf_r,
     az_s,
     az_r,
     cz_s,
@@ -168,6 +176,82 @@
     load_ain.start()
     load_aout.start()
     load_og.start()
+    pl.semaphore_wait(barrier, groups + nz + ny - 3)
+
+    def head_to(src, dst, s, r, device):
+        return remote(
+            src.at[0, :, lanes(device)],
+            dst.at[rows(me), pl.ds(0, HD)],
+            s.at[device],
+            r.at[me],
+            {"sp": device},
+        )
+
+    def own_head(src, dst, r):
+        return pltpu.make_async_copy(
+            src.at[0, :, lanes(me)], dst.at[rows(me), pl.ds(0, HD)], r.at[me]
+        )
+
+    def to_peer(i):
+        return lax.rem(me - i + groups, groups)
+
+    own_head(k_hbm, k_all, k_r).start()
+    each(groups, lambda i: head_to(k_hbm, k_all, k_s, k_r, to_peer(i)).start(), 1)
+
+    half = groups // 2
+    in_rows = HD // nz
+    out_cols = gout_ref.shape[1] // nz
+    side = me // half
+    z_cols = pl.ds(pl.multiple_of(z * out_cols, out_cols), out_cols)
+    z_rows = pl.ds(pl.multiple_of(z * in_rows, in_rows), in_rows)
+
+    def share_device(i):
+        return 2 * lax.rem(chip + i, chips) + side
+
+    def aout_share(device):
+        return remote(
+            aout_cast.at[:, z_cols],
+            aout_all.at[me, :, z_cols],
+            ao_s.at[device],
+            ao_r.at[me],
+            {"sp": device},
+        )
+
+    def ain_share(device):
+        return remote(
+            ain_cast.at[z_rows], ain_all.at[me, z_rows], ai_s.at[device], ai_r.at[me], {"sp": device}
+        )
+
+    load_ain.wait()
+    load_aout.wait()
+    ain_cast[...] = ain_own[...].astype(jnp.bfloat16)
+    aout_cast[...] = aout_own[...].astype(jnp.bfloat16)
+
+    @pl.when(core == side)
+    def _():
+        pltpu.make_async_copy(
+            aout_cast.at[:, z_cols], aout_all.at[me, :, z_cols], ao_r.at[me]
+        ).start()
+        pltpu.make_async_copy(ain_cast.at[z_rows], ain_all.at[me, z_rows], ai_r.at[me]).start()
+
+    @pl.when(core != side)
+    def _():
+        aout_share(partner).start()
+        ain_share(partner).start()
+
+    def send_share(i):
+        aout_share(share_device(i)).start()
+        ain_share(share_device(i)).start()
+
+    each(chips, send_share, 1)
+    own_head(v_hbm, v_all, v_r).start()
+    each(groups, lambda i: head_to(v_hbm, v_all, v_s, v_r, to_peer(i)).start(), 1)
+    own_head(q_hbm, q_all, q_r).start()
+    each(groups, lambda i: head_to(q_hbm, q_all, q_s, q_r, to_peer(i)).start(), 1)
+
+    send_og = remote(og_hbm.at[0], og_all.at[core], og_s, og_r, {"sp": partner})
+    send_og.start()
+
     ends = []
     for j in range(MAX_CLIPS):
         length = jnp.where(count_ref[0] > j, lengths_ref[0, j], 0)
@@ -191,80 +275,6 @@
     each(chips, features)
     mine = me * tok + lax.broadcasted_iota(jnp.int32, (tok, rank), 0)
     live = segment(mine) < MAX_CLIPS
-    load_ain.wait()
-    load_aout.wait()
-    ain_cast[...] = ain_own[...].astype(jnp.bfloat16)
-    aout_cast[...] = aout_own[...].astype(jnp.bfloat16)
-    pl.semaphore_wait(barrier, groups + nz + ny - 3)
-
-    half = groups // 2
-    in_rows = HD // nz
-    out_cols = gout_ref.shape[1] // nz
-    side = me // half
-    z_cols = pl.ds(pl.multiple_of(z * out_cols, out_cols), out_cols)
-    z_rows = pl.ds(pl.multiple_of(z * in_rows, in_rows), in_rows)
-
-    def share_device(i):
-        return 2 * lax.rem(chip + i, chips) + side
-
-    def aout_share(device):
-        return remote(
-            aout_cast.at[:, z_cols],
-            aout_all.at[me, :, z_cols],
-            ao_s.at[device],
-            ao_r.at[me],
-            {"sp": device},
-        )
-
-    def ain_share(device):
-        return remote(
-            ain_cast.at[z_rows], ain_all.at[me, z_rows], ai_s.at[device], ai_r.at[me], {"sp": device}
-        )
-
-    @pl.when(core == side)
-    def _():
-        pltpu.make_async_copy(
-            aout_cast.at[:, z_cols], aout_all.at[me, :, z_cols], ao_r.at[me]
-        ).start()
-        pltpu.make_async_copy(ain_cast.at[z_rows], ain_all.at[me, z_rows], ai_r.at[me]).start()
-
-    @pl.when(core != side)
-    def _():
-        aout_share(partner).start()
-        ain_share(partner).start()
-
-    def send_share(i):
-        aout_share(share_device(i)).start()
-        ain_share(share_device(i)).start()
-
-    each(chips, send_share, 1)
-
-    def head_to(src, dst, s, r, device):
-        return remote(
-            src.at[0, :, lanes(device)],
-            dst.at[rows(me), pl.ds(0, HD)],
-            s.at[device],
-            r.at[me],
-            {"sp": device},
-        )
-
-    def own_head(src, dst, r):
-        return pltpu.make_async_copy(
-            src.at[0, :, lanes(me)], dst.at[rows(me), pl.ds(0, HD)], r.at[me]
-        )
-
-    def to_peer(i):
-        return lax.rem(me - i + groups, groups)
-
-    own_head(k_hbm, k_all, k_r).start()
-    each(groups, lambda i: head_to(k_hbm, k_all, k_s, k_r, to_peer(i)).start(), 1)
-    own_head(v_hbm, v_all, v_r).start()
-    each(groups, lambda i: head_to(v_hbm, v_all, v_s, v_r, to_peer(i)).start(), 1)
-    own_head(q_hbm, q_all, q_r).start()
-    each(groups, lambda i: head_to(q_hbm, q_all, q_s, q_r, to_peer(i)).start(), 1)
-
-    send_og = remote(og_hbm.at[0], og_all.at[core], og_s, og_r, {"sp": partner})
-    send_og.start()
 
     owners = pl.ds(pl.multiple_of(core * half, half), half)
 
@@ -310,27 +320,12 @@
         aout_along(z_peer(i), z_peer(i)).wait_recv()
         ain_along(z_peer(i), z_peer(i)).wait_recv()
 
-    each(nz, wait_along, 1)
     swap_out = remote(
         aout_all.at[owners], aout_all.at[owners], half_s.at[0], half_r.at[0], {"sp": partner}
     )
     swap_in = remote(
         ain_all.at[owners], ain_all.at[owners], half_s.at[1], half_r.at[1], {"sp": partner}
     )
-    swap_out.start()
-    swap_in.start()
-    swap_out.wait_recv()
-    swap_in.wait_recv()
-    load_og.wait()
-
-    outer = jnp.concatenate([aout_all[i].astype(jnp.float32) for i in range(groups)], axis=0)
-    slopes = lax.dot_general(
-        og_all[core],
-        outer.astype(jnp.bfloat16),
-        (((1,), (1,)), ((), ())),
-        preferred_element_type=jnp.float32,
-    ) * rank ** (-0.5)
-    slopes_all[rows(me)] = jnp.where(live, slopes, 0.0).astype(jnp.bfloat16)
 
     def slopes_to(owner, device, slot):
         return remote(
@@ -341,8 +336,26 @@
             {"sp": device},
         )
 
-    slopes_to(me, partner, 0).start()
-    each(chips, lambda i: slopes_to(me, same_core(i), i).start(), 1)
+    def change_cores():
+        each(nz, wait_along, 1)
+        swap_out.start()
+        swap_in.start()
+
+    def spread_slopes():
+        swap_out.wait_recv()
+        swap_in.wait_recv()
+        load_og.wait()
+        outer = jnp.concatenate([aout_all[i].astype(jnp.float32) for i in range(groups)], axis=0)
+        slopes = lax.dot_general(
+            og_all[core],
+            outer.astype(jnp.bfloat16),
+            (((1,), (1,)), ((), ())),
+            preferred_element_type=jnp.float32,
+        ) * rank ** (-0.5)
+        slopes_all[rows(me)] = jnp.where(live, slopes, 0.0).astype(jnp.bfloat16)
+
+        slopes_to(me, partner, 0).start()
+        each(chips, lambda i: slopes_to(me, same_core(i), i).start(), 1)
 
     def wait_head(dst, r, s, peer):
         remote(
@@ -441,14 +454,10 @@
         finish(i + 1, 1)
         give_back(i + 1)
 
-    each(chips // 2 - 1, two_blocks)
-
-    def forward_slopes(i):
-        owner = same_core(i)
-        slopes_to(owner, partner, chips + i).wait_recv()
-        slopes_to(owner, partner, chips + i).start()
-
-    each(chips, forward_slopes, 1)
+    each(chips // 2 - 2, two_blocks)
+    change_cores()
+    each(chips // 2 - 1, two_blocks, chips // 2 - 2)
+    spread_slopes()
 
     wait_queries(chips - 1)
     scores(chips - 1, 1)
@@ -457,10 +466,13 @@
     finish(chips - 1, 1)
     give_back(chips - 1)
 
-    each(chips, lambda i: slopes_to(2 * i + 1 - core, partner, 0).wait_recv())
-    grad_in = lax.dot_general(
-        mixed[...], slopes_all[...], (((0,), (0,)), ((), ())), preferred_element_type=jnp.float32
-    ) * inner ** (-0.5)
+    def forward_slopes(i):
+        owner = same_core(i)
+        slopes_to(owner, partner, chips + i).wait_recv()
+        slopes_to(owner, partner, chips + i).start()
+
+    each(chips, forward_slopes, 1)
+
     out_tiles = out_cols // HD
 
     def y_peer(i):
@@ -502,11 +514,13 @@
             each(nz, lambda i: self.z_copy(z_peer(i), z).start(), 1)
             self.z_in[z] = self.pack[z]
 
-        def across(self):
+        def across(self, more=None):
             each(nz, lambda i: self.z_copy(z_peer(i), z_peer(i)).wait_recv(), 1)
             total = self.z_in[0]
             for p in range(1, nz):
                 total = total + self.z_in[p]
+            if more is not None:
+                total = jnp.concatenate([total, more], axis=0)
             self.y_out[...] = total
             each(ny, lambda i: self.y_copy(y_peer(i), y).start(), 1)
             self.y_in[y] = total
@@ -528,12 +542,6 @@
             each(ny, lambda i: self.y_copy(y_peer(i), y).wait_send(), 1)
             each(nz, lambda i: self.back_copy(z_peer(i), z).wait_send(), 1)
 
-    sum_in = Replicas(in_bufs, in_sems)
-    sum_out = Replicas(out_bufs, out_sems)
-    for p in range(nz):
-        sum_in.pack[p] = grad_in[p * in_rows : (p + 1) * in_rows]
-    sum_in.start()
-
     def wait_mixed(i):
         remote(
             mixed.at[rows(i)], attended.at[:, lanes(i)], o_s.at[i], o_r.at[i], {"sp": partner}
@@ -546,7 +554,6 @@
     adapted_all[core] = jnp.where(live, adapted * inner ** (-0.5), 0.0).astype(jnp.bfloat16)
     send_adapted = remote(adapted_all.at[core], adapted_all.at[core], ad_s, ad_r, {"sp": partner})
     send_adapted.start()
-    sum_in.across()
     send_og.wait_recv()
     send_adapted.wait_recv()
     term_out = lax.dot_general(
@@ -557,42 +564,83 @@
     ) * rank ** (-0.5)
     depth = rank // groups
 
+    chip_tiles = out_tiles - 1
+    chip_cols = chip_tiles * HD * nz
     for j in range(chips):
         at = 2 * j * depth
-        summed[j] = jnp.where(
+        own = jnp.where(
             core == 0, term_out[at : at + depth], term_out[at + depth : at + 2 * depth]
         )
-
-    def chunk_to(i):
-        j = lax.rem(chip + i, chips)
+        summed[j] = own[:, :chip_cols]
+        for p in range(nz):
+            z_first[p, j] = own[:, chip_cols + p * HD : chip_cols + (p + 1) * HD]
+
+    def chunk_to(j, origin):
         return remote(
-            summed.at[j], chip_in.at[chip], chip_s.at[j], chip_r.at[chip], {"sp": 2 * j + core}
-        )
-
-    each(chips, lambda i: chunk_to(i).start(), 1)
+            summed.at[j],
+            chip_in.at[origin],
+            chip_s.at[j],
+            chip_r.at[origin],
+            {"sp": 2 * j + core},
+        )
+
+    def z_first_to(p, origin):
+        return remote(
+            z_first.at[p],
+            z_first_in.at[origin],
+            zf_s.at[p],
+            zf_r.at[origin],
+            {"rep": p * ny + y},
+        )
+
+    def tile_to(j, origin):
+        return remote(
+            tiles.at[j], tile_in.at[origin], ti_s.at[j], ti_r.at[origin], {"sp": 2 * j + core}
+        )
+
+    each(chips, lambda i: chunk_to(chip_of(i), chip).start(), 1)
+    each(nz, lambda i: z_first_to(z_peer(i), z).start(), 1)
     chip_in[chip] = summed[chip]
-
-    def wait_chunk(i):
-        j = lax.rem(chip + i, chips)
-        remote(
-            summed.at[j], chip_in.at[j], chip_s.at[j], chip_r.at[j], {"sp": 2 * j + core}
-        ).wait_recv()
-
+    z_first_in[z] = z_first[z]
+
+    each(chips, lambda i: slopes_to(2 * i + 1 - core, partner, 0).wait_recv())
+    grad_in = lax.dot_general(
+        mixed[...], slopes_all[...], (((0,), (0,)), ((), ())), preferred_element_type=jnp.float32
+    ) * inner ** (-0.5)
+    sum_in = Replicas(in_bufs, in_sems)
+    sum_out = Replicas(out_bufs, out_sems)
+    for p in range(nz):
+        sum_in.pack[p] = grad_in[p * in_rows : (p + 1) * in_rows]
+    sum_in.start()
+
+    each(nz, lambda i: z_first_to(z_peer(i), z_peer(i)).wait_recv(), 1)
+    own = z_first_in[0]
+    for p in range(1, nz):
+        own = own + z_first_in[p]
+    tiles[...] = own
+    each(chips, lambda i: tile_to(chip_of(i), chip).start(), 1)
+    tile_in[chip] = tiles[chip]
+
+    each(chips, lambda i: chunk_to(chip_of(i), chip_of(i)).wait_recv(), 1)
+    own = chip_in[0]
+    for j in range(1, chips):
+        own = own + chip_in[j]
+    for p in range(nz):
+        for t in range(chip_tiles):
+            at = (p * chip_tiles + t) * HD
+            sum_out.pack[p, t * depth : (t + 1) * depth] = own[:, at : at + HD]
+    sum_out.start()
+    sum_in.across()
+    each(chips, lambda i: tile_to(chip_of(i), chip_of(i)).wait_recv(), 1)
+    own = tile_in[0]
+    for j in range(1, chips):
+        own = own + tile_in[j]
+    sum_out.across(own)
     sum_in.back()
-    each(chips, wait_chunk, 1)
-    grad_out = chip_in[0]
-    for j in range(1, chips):
-        grad_out = grad_out + chip_in[j]
-
-    for p in range(nz):
-        for t in range(out_tiles):
-            at = p * out_cols + t * HD
-            sum_out.pack[p, t * 8 : (t + 1) * 8] = grad_out[:, at : at + HD]
-    sum_out.start()
+    sum_out.back()
     sum_in.arrive()
     for p in range(nz):
         gin_ref[p * in_rows : (p + 1) * in_rows] = sum_in.whole[p]
-    sum_out.across()
 
 
     @pl.when(core != side)
@@ -605,7 +653,8 @@
         ain_share(share_device(i)).wait_send()
         slopes_to(me, same_core(i), i).wait_send()
         slopes_to(same_core(i), partner, chips + i).wait_send()
-        chunk_to(i).wait_send()
+        chunk_to(chip_of(i), chip).wait_send()
+        tile_to(chip_of(i), chip).wait_send()
 
     each(chips, sent_to_chips, 1)
     slopes_to(me, partner, 0).wait_send()
@@ -617,6 +666,7 @@
     def sent_along(i):
         aout_along(z_peer(i), z).wait_send()
         ain_along(z_peer(i), z).wait_send()
+        z_first_to(z_peer(i), z).wait_send()
 
     each(nz, sent_along, 1)
 
@@ -628,14 +678,15 @@
         mixed_to(peer).wait_send()
 
     each(groups, sent_to_group, 1)
-    sum_out.back()
     sum_in.sent()
     sum_out.sent()
     sum_out.arrive()
     for p in range(nz):
-        for t in range(out_tiles):
-            at = p * out_cols + t * HD
-            gout_ref[:, at : at + HD] = sum_out.whole[p, t * 8 : (t + 1) * 8]
+        for t in range(chip_tiles):
+            at = (p * chip_tiles + t) * HD
+            gout_ref[:, at : at + HD] = sum_out.whole[p, t * depth : (t + 1) * depth]
+        at = chip_cols + p * HD
+        gout_ref[:, at : at + HD] = sum_out.whole[p, chip_tiles * depth :]
 
 
 def adamw_kernel(*refs):
@@ -670,17 +721,17 @@
     nz = reps // ny
     tokens = tok * groups
     depth = rank // groups
-    in_lines, out_lines = HD // nz, (width // nz // HD) * 8
+    in_lines, out_lines = HD // nz, (width // nz // HD) * depth
     bf16, f32 = jnp.bfloat16, jnp.float32
     vmem = pl.BlockSpec(memory_space=pltpu.VMEM)
     smem = pl.BlockSpec(memory_space=pltpu.SMEM)
     hbm = pl.BlockSpec(memory_space=pl.ANY)
     dma = pltpu.SemaphoreType.DMA
 
-    def sum_bufs(lines):
+    def sum_bufs(first, lines):
         return [
-            pltpu.VMEM((nz, lines, HD), f32),
-            pltpu.VMEM((nz, lines, HD), f32),
+            pltpu.VMEM((nz, first, HD), f32),
+            pltpu.VMEM((nz, first, HD), f32),
             pltpu.VMEM((lines, HD), f32),
             pltpu.VMEM((ny, lines, HD), f32),
             pltpu.VMEM((lines, HD), f32),
@@ -714,16 +765,20 @@
             pltpu.VMEM((groups, depth, width), bf16),
             pltpu.VMEM((tokens, rank), bf16),
             pltpu.VMEM((2, tok, rank), bf16),
-            pltpu.VMEM((chips, depth, width), f32),
-            pltpu.VMEM((chips, depth, width), f32),
-            sum_bufs(in_lines),
-            sum_bufs(out_lines),
+            pltpu.VMEM((chips, depth, width - nz * HD), f32),
+            pltpu.VMEM((chips, depth, width - nz * HD), f32),
+            pltpu.VMEM((nz, chips, depth, HD), f32),
+            pltpu.VMEM((nz, chips, depth, HD), f32),
+            pltpu.VMEM((chips, depth, HD), f32),
+            pltpu.VMEM((chips, depth, HD), f32),
+            sum_bufs(in_lines, in_lines),
+            sum_bufs(out_lines - depth, out_lines),
             dma((3,)),
         ]
         + [dma(())] * 4
         + [dma((groups,))] * 14
-        + [dma((chips,))] * 2
-        + [dma((nz,))] * 4
+        + [dma((chips,))] * 4
+        + [dma((nz,))] * 6
         + [dma((2,))] * 2
         + [sum_sems, sum_sems],
         compiler_params=pltpu.CompilerParams(

time: 99.6 us -> 101 us (1.014)
  Pallas kernels: 98.1 us -> 99.7 us
    pallas_call x1, Pallas kernels: 96.1 us -> 97.7 us  [per_device(): pl.pallas_call(functools.partial(step_kernel, (tok, groups, nz, ny)), nam...]
where the time goes in v2:
time: 101 us
  Pallas kernels  99.7 us (99%)
  between operations  1.29 us (1%)
    pallas_call x1, Pallas kernels, per_device(): pl.pallas_call(functools.partial(step_kernel, (tok, groups, nz, ny)), nam...  97.7 us

profile of v2, /device:TPU:6, one launch (start us, length us, event | category | flops | bytes accessed | tf_op | source)
XLA Modules:
  0.0 101.0 jit_solution(953614485870166703)
XLA Ops:
  1.3 97.7 %adapter_step.1 = (f32[128,128]{1,0:T(8,128)}, f32[8,3072]{1,0:T(8,128)}) custom-call(s32[1]{0:T(128)S(6)} %copy.18.count_ref, s32[1,3]{1,0:T(1,128)} %lengths_ref.1, bf16[1,192,2048]{2,1,0:T(8,128)(2,1)} %q_hbm.1, bf16[1,192,2048]{2,1,0:T(8,128)(2,1)} %k_hbm.1, bf16[1,192,2048]{2,1,0:T(8,128)(2,1)} %v_hbm.1, bf16[1,192,3072]{2,1,0:T(8,128)(2,1)} %og_hbm.1, ...), custom_call_target="tpu_custom_call" | custom-call | tf_op jit(solution)/shard_map/adapter_step/pallas_call | solution.py:742
  99.0 2.0 %adamw.1 = (f32[128,128]{1,0:T(8,128)}, f32[128,128]{1,0:T(8,128)}, f32[128,128]{1,0:T(8,128)}, f32[8,3072]{1,0:T(8,128)}, f32[8,3072]{1,0:T(8,128)}, /*index=5*/f32[8,3072]{1,0:T(8,128)}) custom-call(f32[128,128]{1,0:T(8,128)} %refs_0_.1, f32[128,128]{1,0:T(8,128)} %get-tuple-element.8.refs_1_, f32[128,128]{1,0:T(8,128)} %refs_2_.1, f32[128,128]{1,0:T(8,128)} %refs_3_.1, ...), custom_call_target="tpu_custom_call" | custom-call | tf_op jit(solution)/shard_map/adamw/pallas_call | solution.py:798

commit v3 on v2

--- a/solution.py
+++ b/solution.py
@@ -21,6 +21,9 @@
 EXP2_SCALE = HD ** (-0.5) * math.log2(math.e)
 MASK = -131072.0
 KEY_CHUNKS = 4
+EARLY_CHIPS = 5
+MORE = 3
+ROWS = 64
 
 
 def adamw(param, grad, moment, square):
@@ -41,6 +44,10 @@
         device_id=device,
         device_id_type=MESH,
     )
+
+
+def drain(ref, sem):
+    pltpu.make_async_copy(ref, ref, sem).wait()
 
 
 def each(n, body, start=0):
@@ -68,6 +75,8 @@
     v_all,
     scores_buf,
     high_buf,
+    weights,
+    totals,
     mixed,
     attended,
     og_all,
@@ -106,6 +115,8 @@
     ao_r,
     sl_s,
     sl_r,
+    pass_s,
+    pass_r,
     chip_s,
     chip_r,
     ti_s,
@@ -182,21 +193,19 @@
         return remote(
             src.at[0, :, lanes(device)],
             dst.at[rows(me), pl.ds(0, HD)],
-            s.at[device],
-            r.at[me],
+            s,
+            r,
             {"sp": device},
         )
 
     def own_head(src, dst, r):
         return pltpu.make_async_copy(
-            src.at[0, :, lanes(me)], dst.at[rows(me), pl.ds(0, HD)], r.at[me]
+            src.at[0, :, lanes(me)], dst.at[rows(me), pl.ds(0, HD)], r
         )
 
     def to_peer(i):
         return lax.rem(me - i + groups, groups)
 
-    own_head(k_hbm, k_all, k_r).start()
-    each(groups, lambda i: head_to(k_hbm, k_all, k_s, k_r, to_peer(i)).start(), 1)
 
     half = groups // 2
     in_rows = HD // nz
@@ -212,14 +221,14 @@
         return remote(
             aout_cast.at[:, z_cols],
             aout_all.at[me, :, z_cols],
-            ao_s.at[device],
-            ao_r.at[me],
+            ao_s,
+            ao_r,
             {"sp": device},
         )
 
     def ain_share(device):
         return remote(
-            ain_cast.at[z_rows], ain_all.at[me, z_rows], ai_s.at[device], ai_r.at[me], {"sp": device}
+            ain_cast.at[z_rows], ain_all.at[me, z_rows], ai_s, ai_r, {"sp": device}
         )
 
     load_ain.wait()
@@ -230,9 +239,9 @@
     @pl.when(core == side)
     def _():
         pltpu.make_async_copy(
-            aout_cast.at[:, z_cols], aout_all.at[me, :, z_cols], ao_r.at[me]
+            aout_cast.at[:, z_cols], aout_all.at[me, :, z_cols], ao_r
         ).start()
-        pltpu.make_async_copy(ain_cast.at[z_rows], ain_all.at[me, z_rows], ai_r.at[me]).start()
+        pltpu.make_async_copy(ain_cast.at[z_rows], ain_all.at[me, z_rows], ai_r).start()
 
     @pl.when(core != side)
     def _():
@@ -244,10 +253,24 @@
         ain_share(share_device(i)).start()
 
     each(chips, send_share, 1)
+
+    def to_chip(src, dst, send, recv, j):
+        for c in range(2):
+            head_to(src, dst, send, recv, 2 * lax.rem(chip - j + chips, chips) + c).start()
+
+    def queries_to(j):
+        to_chip(q_hbm, q_all, q_s, q_r.at[chip], j)
+
+    def values_to(j):
+        to_chip(v_hbm, v_all, v_s, v_r, j)
+
+    own_head(k_hbm, k_all, k_r).start()
+    each(groups, lambda i: head_to(k_hbm, k_all, k_s, k_r, to_peer(i)).start(), 1)
+    own_head(q_hbm, q_all, q_r.at[chip]).start()
     own_head(v_hbm, v_all, v_r).start()
-    each(groups, lambda i: head_to(v_hbm, v_all, v_s, v_r, to_peer(i)).start(), 1)
-    own_head(q_hbm, q_all, q_r).start()
-    each(groups, lambda i: head_to(q_hbm, q_all, q_s, q_r, to_peer(i)).start(), 1)
+    head_to(q_hbm, q_all, q_s, q_r.at[chip], partner).start()
+    head_to(v_hbm, v_all, v_s, v_r, partner).start()
+    queries_to(1)
 
     send_og = remote(og_hbm.at[0], og_all.at[core], og_s, og_r, {"sp": partner})
     send_og.start()
@@ -278,24 +301,8 @@
 
     owners = pl.ds(pl.multiple_of(core * half, half), half)
 
-    def wait_share(i):
-        owner = core * half + i
-        remote(
-            aout_cast.at[:, z_cols],
-            aout_all.at[owner, :, z_cols],
-            ao_s.at[owner],
-            ao_r.at[owner],
-            {"sp": partner},
-        ).wait_recv()
-        remote(
-            ain_cast.at[z_rows],
-            ain_all.at[owner, z_rows],
-            ai_s.at[owner],
-            ai_r.at[owner],
-            {"sp": partner},
-        ).wait_recv()
-
-    each(half, wait_share)
+    drain(aout_all.at[owners, :, z_cols], ao_r)
+    drain(ain_all.at[owners, z_rows], ai_r)
 
     def z_peer(i):
         return lax.rem(z + i, nz)
@@ -303,12 +310,12 @@
     def aout_along(p, origin):
         cols = pl.ds(pl.multiple_of(origin * out_cols, out_cols), out_cols)
         part = aout_all.at[owners, :, cols]
-        return remote(part, part, az_s.at[p], az_r.at[origin], {"rep": p * ny + y})
+        return remote(part, part, az_s, az_r, {"rep": p * ny + y})
 
     def ain_along(p, origin):
         lines = pl.ds(pl.multiple_of(origin * in_rows, in_rows), in_rows)
         part = ain_all.at[owners, lines]
-        return remote(part, part, cz_s.at[p], cz_r.at[origin], {"rep": p * ny + y})
+        return remote(part, part, cz_s, cz_r, {"rep": p * ny + y})
 
     def send_along(i):
         aout_along(z_peer(i), z).start()
@@ -316,9 +323,8 @@
 
     each(nz, send_along, 1)
 
-    def wait_along(i):
-        aout_along(z_peer(i), z_peer(i)).wait_recv()
-        ain_along(z_peer(i), z_peer(i)).wait_recv()
+    others = aout_all.at[owners, :, pl.ds(0, (nz - 1) * out_cols)]
+    other_lines = ain_all.at[owners, pl.ds(0, (nz - 1) * in_rows)]
 
     swap_out = remote(
         aout_all.at[owners], aout_all.at[owners], half_s.at[0], half_r.at[0], {"sp": partner}
@@ -327,21 +333,17 @@
         ain_all.at[owners], ain_all.at[owners], half_s.at[1], half_r.at[1], {"sp": partner}
     )
 
-    def slopes_to(owner, device, slot):
-        return remote(
-            slopes_all.at[rows(owner)],
-            slopes_all.at[rows(owner)],
-            sl_s.at[slot],
-            sl_r.at[owner],
-            {"sp": device},
-        )
+    def slopes_to(owner, device, s, r):
+        part = slopes_all.at[rows(owner)]
+        return remote(part, part, s, r, {"sp": device})
 
     def change_cores():
-        each(nz, wait_along, 1)
+        drain(others, az_r)
+        drain(other_lines, cz_r)
         swap_out.start()
         swap_in.start()
 
-    def spread_slopes():
+    def make_slopes():
         swap_out.wait_recv()
         swap_in.wait_recv()
         load_og.wait()
@@ -354,20 +356,19 @@
         ) * rank ** (-0.5)
         slopes_all[rows(me)] = jnp.where(live, slopes, 0.0).astype(jnp.bfloat16)
 
-        slopes_to(me, partner, 0).start()
-        each(chips, lambda i: slopes_to(me, same_core(i), i).start(), 1)
-
-    def wait_head(dst, r, s, peer):
-        remote(
-            dst.at[rows(peer), pl.ds(0, HD)],
-            dst.at[rows(peer), pl.ds(0, HD)],
-            s.at[peer],
-            r.at[peer],
-            {"sp": partner},
-        ).wait_recv()
-
-    each(groups, lambda i: wait_head(k_all, k_r, k_s, i))
-    each(groups, lambda i: wait_head(v_all, v_r, v_s, i))
+    def spread_slopes():
+        slopes_to(me, partner, sl_s, pass_r).start()
+        each(chips, lambda i: slopes_to(me, same_core(i), sl_s, sl_r).start(), 1)
+
+    drain(k_all.at[pl.ds(0, tokens - tok), pl.ds(0, HD)], k_s)
+    each(EARLY_CHIPS, queries_to, 2)
+
+    def send_more(n):
+        pl.when(n < chips - EARLY_CHIPS)(lambda: queries_to(EARLY_CHIPS + n))
+        j = n - (chips - EARLY_CHIPS) + 1
+        pl.when((j >= 1) & (j < chips))(lambda: values_to(j))
+
+    drain(k_all.at[:, pl.ds(0, HD)], k_r)
 
     def chip_of(i):
         return lax.rem(chip + i, chips)
@@ -376,8 +377,7 @@
         return pl.ds(pl.multiple_of(chip_of(i) * block, block), block)
 
     def wait_queries(i):
-        wait_head(q_all, q_r, q_s, 2 * chip_of(i))
-        wait_head(q_all, q_r, q_s, 2 * chip_of(i) + 1)
+        drain(q_all.at[block_rows(i), pl.ds(0, HD)], q_r.at[chip_of(i)])
 
     width = tokens // KEY_CHUNKS
 
@@ -397,36 +397,40 @@
                 high = piece if high is None else jnp.maximum(high, piece)
         high_buf[slot] = jnp.broadcast_to(jnp.max(high, axis=1, keepdims=True), (block, HD))
 
-    def finish(i, slot):
-        high = high_buf[slot][:, :1]
-        total = None
-        row_total = None
-        for c in range(KEY_CHUNKS):
-            s = scores_buf[slot, :, c * width : (c + 1) * width]
-            exponent = jnp.exp2((s - high) * EXP2_SCALE)
-            for j in range(width // HD):
-                piece = exponent[:, j * HD : (j + 1) * HD]
-                row_total = piece if row_total is None else row_total + piece
-            term = jnp.dot(
-                exponent.astype(jnp.bfloat16),
-                v_all[c * width : (c + 1) * width, :],
-                preferred_element_type=jnp.float32,
+    def weigh(i, slot):
+        at = pl.multiple_of(chip_of(i) * block, block)
+        for g in range(block // ROWS):
+            lines = slice(g * ROWS, (g + 1) * ROWS)
+            high = high_buf[slot, lines]
+            row_total = None
+            for j in range(tokens // HD):
+                s = scores_buf[slot, lines, j * HD : (j + 1) * HD]
+                exponent = jnp.exp2((s - high) * EXP2_SCALE)
+                row_total = exponent if row_total is None else row_total + exponent
+                weights[pl.ds(at + g * ROWS, ROWS), j * HD : (j + 1) * HD] = exponent.astype(
+                    jnp.bfloat16
+                )
+            totals[pl.ds(at + g * ROWS, ROWS), :] = jnp.broadcast_to(
+                jnp.sum(row_total, axis=1, keepdims=True), (ROWS, HD)
             )
-            total = term if total is None else total + term
-        row_total = jnp.sum(row_total, axis=1, keepdims=True)
-        mixed[block_rows(i), :] = (total / row_total).astype(jnp.bfloat16)
+
+    def mix(i):
+        product = jnp.dot(
+            weights[block_rows(i), :], v_all[...], preferred_element_type=jnp.float32
+        )
+        mixed[block_rows(i), :] = (product / totals[block_rows(i), :]).astype(jnp.bfloat16)
 
     def mixed_to(device):
         return remote(
             mixed.at[rows(device)],
             attended.at[:, lanes(me)],
-            o_s.at[device],
-            o_r.at[me],
+            o_s,
+            o_r,
             {"sp": device},
         )
 
     def own_mixed():
-        return pltpu.make_async_copy(mixed.at[rows(me)], attended.at[:, lanes(me)], o_r.at[me])
+        return pltpu.make_async_copy(mixed.at[rows(me)], attended.at[:, lanes(me)], o_r)
 
     def give_back(i):
         for c in range(2):
@@ -445,33 +449,32 @@
 
     def two_blocks(t):
         i = 2 * t
+        each(MORE, lambda n: send_more(MORE * i + n))
         wait_queries(i + 1)
         scores(i + 1, 1)
-        finish(i, 0)
-        give_back(i)
+        weigh(i, 0)
+        each(MORE, lambda n: send_more(MORE * i + MORE + n))
         wait_queries(i + 2)
         scores(i + 2, 0)
-        finish(i + 1, 1)
-        give_back(i + 1)
-
-    each(chips // 2 - 2, two_blocks)
-    change_cores()
-    each(chips // 2 - 1, two_blocks, chips // 2 - 2)
-    spread_slopes()
-
+        weigh(i + 1, 1)
+
+    each(chips // 2 - 1, two_blocks)
     wait_queries(chips - 1)
     scores(chips - 1, 1)
-    finish(chips - 2, 0)
-    give_back(chips - 2)
-    finish(chips - 1, 1)
-    give_back(chips - 1)
-
-    def forward_slopes(i):
-        owner = same_core(i)
-        slopes_to(owner, partner, chips + i).wait_recv()
-        slopes_to(owner, partner, chips + i).start()
-
-    each(chips, forward_slopes, 1)
+    weigh(chips - 2, 0)
+    change_cores()
+    weigh(chips - 1, 1)
+    make_slopes()
+    drain(v_all, v_r)
+
+    def mix_block(n):
+        i = lax.rem(n + 1, chips)
+        mix(i)
+        give_back(i)
+
+    each(chips, mix_block)
+    drain(mixed.at[pl.ds(0, tokens - tok)], o_s)
+    spread_slopes()
 
     out_tiles = out_cols // HD
 
@@ -487,8 +490,8 @@
             return remote(
                 self.pack.at[p],
                 self.z_in.at[origin],
-                self.zi_s.at[p],
-                self.zi_r.at[origin],
+                self.zi_s,
+                self.zi_r,
                 {"rep": p * ny + y},
             )
 
@@ -496,8 +499,8 @@
             return remote(
                 self.y_out,
                 self.y_in.at[origin],
-                self.y_s.at[p],
-                self.y_r.at[origin],
+                self.y_s,
+                self.y_r,
                 {"rep": z * ny + p},
             )
 
@@ -505,8 +508,8 @@
             return remote(
                 self.z_out,
                 self.whole.at[origin],
-                self.zo_s.at[p],
-                self.zo_r.at[origin],
+                self.zo_s,
+                self.zo_r,
                 {"rep": p * ny + y},
             )
 
@@ -515,7 +518,7 @@
             self.z_in[z] = self.pack[z]
 
         def across(self, more=None):
-            each(nz, lambda i: self.z_copy(z_peer(i), z_peer(i)).wait_recv(), 1)
+            drain(self.z_in.at[pl.ds(0, nz - 1)], self.zi_r)
             total = self.z_in[0]
             for p in range(1, nz):
                 total = total + self.z_in[p]
@@ -526,7 +529,7 @@
             self.y_in[y] = total
 
         def back(self):
-            each(ny, lambda i: self.y_copy(y_peer(i), y_peer(i)).wait_recv(), 1)
+            drain(self.y_in.at[pl.ds(0, ny - 1)], self.y_r)
             total = self.y_in[0]
             for p in range(1, ny):
                 total = total + self.y_in[p]
@@ -535,19 +538,14 @@
             self.whole[z] = total
 
         def arrive(self):
-            each(nz, lambda i: self.back_copy(z_peer(i), z_peer(i)).wait_recv(), 1)
+            drain(self.whole.at[pl.ds(0, nz - 1)], self.zo_r)
 
         def sent(self):
-            each(nz, lambda i: self.z_copy(z_peer(i), z).wait_send(), 1)
-            each(ny, lambda i: self.y_copy(y_peer(i), y).wait_send(), 1)
-            each(nz, lambda i: self.back_copy(z_peer(i), z).wait_send(), 1)
-
-    def wait_mixed(i):
-        remote(
-            mixed.at[rows(i)], attended.at[:, lanes(i)], o_s.at[i], o_r.at[i], {"sp": partner}
-        ).wait_recv()
-
-    each(groups, wait_mixed)
+            drain(self.pack.at[pl.ds(0, nz - 1)], self.zi_s)
+            drain(self.y_in.at[pl.ds(0, ny - 1)], self.y_s)
+            drain(self.whole.at[pl.ds(0, nz - 1)], self.zo_s)
+
+    drain(attended, o_r)
     adapted = jnp.dot(
         attended[...], ain_all[...].reshape(inner, rank), preferred_element_type=jnp.float32
     )
@@ -579,8 +577,8 @@
         return remote(
             summed.at[j],
             chip_in.at[origin],
-            chip_s.at[j],
-            chip_r.at[origin],
+            chip_s,
+            chip_r,
             {"sp": 2 * j + core},
         )
 
@@ -588,14 +586,14 @@
         return remote(
             z_first.at[p],
             z_first_in.at[origin],
-            zf_s.at[p],
-            zf_r.at[origin],
+            zf_s,
+            zf_r,
             {"rep": p * ny + y},
         )
 
     def tile_to(j, origin):
         return remote(
-            tiles.at[j], tile_in.at[origin], ti_s.at[j], ti_r.at[origin], {"sp": 2 * j + core}
+            tiles.at[j], tile_in.at[origin], ti_s, ti_r, {"sp": 2 * j + core}
         )
 
     each(chips, lambda i: chunk_to(chip_of(i), chip).start(), 1)
@@ -603,7 +601,18 @@
     chip_in[chip] = summed[chip]
     z_first_in[z] = z_first[z]
 
-    each(chips, lambda i: slopes_to(2 * i + 1 - core, partner, 0).wait_recv())
+    drain(slopes_all.at[pl.ds(0, (chips - 1) * tok)], sl_r)
+    each(chips, lambda i: slopes_to(same_core(i), partner, pass_s, pass_r).start(), 1)
+
+    drain(z_first_in.at[pl.ds(0, nz - 1)], zf_r)
+    own = z_first_in[0]
+    for p in range(1, nz):
+        own = own + z_first_in[p]
+    tiles[...] = own
+    each(chips, lambda i: tile_to(chip_of(i), chip).start(), 1)
+    tile_in[chip] = tiles[chip]
+
+    drain(slopes_all.at[pl.ds(0, chips * tok)], pass_r)
     grad_in = lax.dot_general(
         mixed[...], slopes_all[...], (((0,), (0,)), ((), ())), preferred_element_type=jnp.float32
     ) * inner ** (-0.5)
@@ -613,15 +622,7 @@
         sum_in.pack[p] = grad_in[p * in_rows : (p + 1) * in_rows]
     sum_in.start()
 
-    each(nz, lambda i: z_first_to(z_peer(i), z_peer(i)).wait_recv(), 1)
-    own = z_first_in[0]
-    for p in range(1, nz):
-        own = own + z_first_in[p]
-    tiles[...] = own
-    each(chips, lambda i: tile_to(chip_of(i), chip).start(), 1)
-    tile_in[chip] = tiles[chip]
-
-    each(chips, lambda i: chunk_to(chip_of(i), chip_of(i)).wait_recv(), 1)
+    drain(chip_in.at[pl.ds(0, chips - 1)], chip_r)
     own = chip_in[0]
     for j in range(1, chips):
         own = own + chip_in[j]
@@ -631,7 +632,7 @@
             sum_out.pack[p, t * depth : (t + 1) * depth] = own[:, at : at + HD]
     sum_out.start()
     sum_in.across()
-    each(chips, lambda i: tile_to(chip_of(i), chip_of(i)).wait_recv(), 1)
+    drain(tile_in.at[pl.ds(0, chips - 1)], ti_r)
     own = tile_in[0]
     for j in range(1, chips):
         own = own + tile_in[j]
@@ -642,42 +643,29 @@
     for p in range(nz):
         gin_ref[p * in_rows : (p + 1) * in_rows] = sum_in.whole[p]
 
-
     @pl.when(core != side)
     def _():
-        aout_share(partner).wait_send()
-        ain_share(partner).wait_send()
-
-    def sent_to_chips(i):
-        aout_share(share_device(i)).wait_send()
-        ain_share(share_device(i)).wait_send()
-        slopes_to(me, same_core(i), i).wait_send()
-        slopes_to(same_core(i), partner, chips + i).wait_send()
-        chunk_to(chip_of(i), chip).wait_send()
-        tile_to(chip_of(i), chip).wait_send()
-
-    each(chips, sent_to_chips, 1)
-    slopes_to(me, partner, 0).wait_send()
+        drain(aout_all.at[pl.ds(0, chips), :, z_cols], ao_s)
+        drain(ain_all.at[pl.ds(0, chips), z_rows], ai_s)
+
+    @pl.when(core == side)
+    def _():
+        drain(aout_all.at[pl.ds(0, chips - 1), :, z_cols], ao_s)
+        drain(ain_all.at[pl.ds(0, chips - 1), z_rows], ai_s)
+
+    drain(q_all.at[pl.ds(0, tokens - tok), pl.ds(0, HD)], q_s)
+    drain(v_all.at[pl.ds(0, tokens - tok)], v_s)
+    drain(others, az_s)
+    drain(other_lines, cz_s)
+    drain(slopes_all.at[pl.ds(0, chips * tok)], sl_s)
+    drain(slopes_all.at[pl.ds(0, (chips - 1) * tok)], pass_s)
+    drain(chip_in.at[pl.ds(0, chips - 1)], chip_s)
+    drain(tile_in.at[pl.ds(0, chips - 1)], ti_s)
+    drain(z_first_in.at[pl.ds(0, nz - 1)], zf_s)
     send_og.wait_send()
     send_adapted.wait_send()
     swap_out.wait_send()
     swap_in.wait_send()
-
-    def sent_along(i):
-        aout_along(z_peer(i), z).wait_send()
-        ain_along(z_peer(i), z).wait_send()
-        z_first_to(z_peer(i), z).wait_send()
-
-    each(nz, sent_along, 1)
-
-    def sent_to_group(i):
-        peer = to_peer(i)
-        head_to(k_hbm, k_all, k_s, k_r, peer).wait_send()
-        head_to(v_hbm, v_all, v_s, v_r, peer).wait_send()
-        head_to(q_hbm, q_all, q_s, q_r, peer).wait_send()
-        mixed_to(peer).wait_send()
-
-    each(groups, sent_to_group, 1)
     sum_in.sent()
     sum_out.sent()
     sum_out.arrive()
@@ -738,7 +726,7 @@
             pltpu.VMEM((nz, lines, HD), f32),
         ]
 
-    sum_sems = [dma((n,)) for n in (nz, nz, ny, ny, nz, nz)]
+    sum_sems = [dma(())] * 6
     grad_in, grad_out = pl.pallas_call(
         functools.partial(step_kernel, (tok, groups, nz, ny)),
         name="adapter_step",
@@ -754,6 +742,8 @@
             pltpu.VMEM((tokens, HD), bf16),
             pltpu.VMEM((2, 2 * tok, tokens), f32),
             pltpu.VMEM((2, 2 * tok, HD), f32),
+            pltpu.VMEM((tokens, tokens), bf16),
+            pltpu.VMEM((tokens, HD), f32),
             pltpu.VMEM((tokens, HD), bf16),
             pltpu.VMEM((tok, groups * HD), bf16),
             pltpu.VMEM((2, tok, width), bf16),
@@ -775,10 +765,9 @@
             sum_bufs(out_lines - depth, out_lines),
             dma((3,)),
         ]
-        + [dma(())] * 4
-        + [dma((groups,))] * 14
-        + [dma((chips,))] * 4
-        + [dma((nz,))] * 6
+        + [dma(())] * 9
+        + [dma((chips,))]
+        + [dma(())] * 20
         + [dma((2,))] * 2
         + [sum_sems, sum_sems],
         compiler_params=pltpu.CompilerParams(

time: 101 us -> 92.9 us (0.920)
  Pallas kernels: 99.7 us -> 91.4 us
    pallas_call x1, Pallas kernels: 97.7 us -> 89.4 us  [per_device(): pl.pallas_call(functools.partial(step_kernel, (tok, groups, nz, ny)), nam...]
where the time goes in v3:
time: 92.9 us; the launch traced here: 92.7 us
  Pallas kernels  91.4 us (98%)
  between operations  1.29 us (1%)
    pallas_call x1, Pallas kernels, per_device(): pl.pallas_call(functools.partial(step_kernel, (tok, groups, nz, ny)), nam...  89.4 us
    pallas_call x1, Pallas kernels, per_device(): pl.pallas_call(adamw_kernel, name='adamw', out_shape=[jax.ShapeDtypeStruc...  1.99 us

profile of v3, /device:TPU:6, one launch (start us, length us, event | category | flops | bytes accessed | tf_op | source)
XLA Modules:
  0.0 92.7 jit_solution(11647584093527396885)
XLA Ops:
  1.3 89.4 %adapter_step.1 = (f32[128,128]{1,0:T(8,128)}, f32[8,3072]{1,0:T(8,128)}) custom-call(s32[1]{0:T(128)S(6)} %copy.18.count_ref, s32[1,3]{1,0:T(1,128)} %lengths_ref.1, bf16[1,192,2048]{2,1,0:T(8,128)(2,1)} %q_hbm.1, bf16[1,192,2048]{2,1,0:T(8,128)(2,1)} %k_hbm.1, bf16[1,192,2048]{2,1,0:T(8,128)(2,1)} %v_hbm.1, bf16[1,192,3072]{2,1,0:T(8,128)(2,1)} %og_hbm.1, ...), custom_call_target="tpu_custom_call" | custom-call | tf_op jit(solution)/shard_map/adapter_step/pallas_call | solution.py:730
  90.7 2.0 %adamw.1 = (f32[128,128]{1,0:T(8,128)}, f32[128,128]{1,0:T(8,128)}, f32[128,128]{1,0:T(8,128)}, f32[8,3072]{1,0:T(8,128)}, f32[8,3072]{1,0:T(8,128)}, /*index=5*/f32[8,3072]{1,0:T(8,128)}) custom-call(f32[128,128]{1,0:T(8,128)} %refs_0_.1, f32[128,128]{1,0:T(8,128)} %get-tuple-element.8.refs_1_, f32[128,128]{1,0:T(8,128)} %refs_2_.1, f32[128,128]{1,0:T(8,128)} %refs_3_.1, ...), custom_call_target="tpu_custom_call" | custom-call | tf_op jit(solution)/shard_map/adamw/pallas_call | solution.py:787

commit v4 on v3

--- a/solution.py
+++ b/solution.py
@@ -457,24 +457,25 @@
         wait_queries(i + 2)
         scores(i + 2, 0)
         weigh(i + 1, 1)
+        pl.when(t == 1)(change_cores)
 
     each(chips // 2 - 1, two_blocks)
+    make_slopes()
+    spread_slopes()
     wait_queries(chips - 1)
     scores(chips - 1, 1)
     weigh(chips - 2, 0)
-    change_cores()
     weigh(chips - 1, 1)
-    make_slopes()
-    drain(v_all, v_r)
-
-    def mix_block(n):
-        i = lax.rem(n + 1, chips)
+
+    def mix_block(i):
         mix(i)
         give_back(i)
 
-    each(chips, mix_block)
-    drain(mixed.at[pl.ds(0, tokens - tok)], o_s)
-    spread_slopes()
+    drain(v_all, v_r)
+    each(chips + 1, lambda n: mix_block(lax.rem(n, chips)), 1)
+
+    drain(slopes_all.at[pl.ds(0, (chips - 1) * tok)], sl_r)
+    each(chips, lambda i: slopes_to(same_core(i), partner, pass_s, pass_r).start(), 1)
 
     out_tiles = out_cols // HD
 
@@ -544,6 +545,16 @@
             drain(self.pack.at[pl.ds(0, nz - 1)], self.zi_s)
             drain(self.y_in.at[pl.ds(0, ny - 1)], self.y_s)
             drain(self.whole.at[pl.ds(0, nz - 1)], self.zo_s)
+
+    drain(slopes_all.at[pl.ds(0, chips * tok)], pass_r)
+    grad_in = lax.dot_general(
+        mixed[...], slopes_all[...], (((0,), (0,)), ((), ())), preferred_element_type=jnp.float32
+    ) * inner ** (-0.5)
+    sum_in = Replicas(in_bufs, in_sems)
+    sum_out = Replicas(out_bufs, out_sems)
+    for p in range(nz):
+        sum_in.pack[p] = grad_in[p * in_rows : (p + 1) * in_rows]
+    sum_in.start()
 
     drain(attended, o_r)
     adapted = jnp.dot(
@@ -601,9 +612,7 @@
     chip_in[chip] = summed[chip]
     z_first_in[z] = z_first[z]
 
-    drain(slopes_all.at[pl.ds(0, (chips - 1) * tok)], sl_r)
-    each(chips, lambda i: slopes_to(same_core(i), partner, pass_s, pass_r).start(), 1)
-
+    sum_in.across()
     drain(z_first_in.at[pl.ds(0, nz - 1)], zf_r)
     own = z_first_in[0]
     for p in range(1, nz):
@@ -611,16 +620,6 @@
     tiles[...] = own
     each(chips, lambda i: tile_to(chip_of(i), chip).start(), 1)
     tile_in[chip] = tiles[chip]
-
-    drain(slopes_all.at[pl.ds(0, chips * tok)], pass_r)
-    grad_in = lax.dot_general(
-        mixed[...], slopes_all[...], (((0,), (0,)), ((), ())), preferred_element_type=jnp.float32
-    ) * inner ** (-0.5)
-    sum_in = Replicas(in_bufs, in_sems)
-    sum_out = Replicas(out_bufs, out_sems)
-    for p in range(nz):
-        sum_in.pack[p] = grad_in[p * in_rows : (p + 1) * in_rows]
-    sum_in.start()
 
     drain(chip_in.at[pl.ds(0, chips - 1)], chip_r)
     own = chip_in[0]
@@ -631,17 +630,16 @@
             at = (p * chip_tiles + t) * HD
             sum_out.pack[p, t * depth : (t + 1) * depth] = own[:, at : at + HD]
     sum_out.start()
-    sum_in.across()
+    sum_in.back()
     drain(tile_in.at[pl.ds(0, chips - 1)], ti_r)
     own = tile_in[0]
     for j in range(1, chips):
         own = own + tile_in[j]
     sum_out.across(own)
-    sum_in.back()
-    sum_out.back()
     sum_in.arrive()
     for p in range(nz):
         gin_ref[p * in_rows : (p + 1) * in_rows] = sum_in.whole[p]
+    sum_out.back()
 
     @pl.when(core != side)
     def _():
@@ -654,6 +652,7 @@
         drain(ain_all.at[pl.ds(0, chips - 1), z_rows], ai_s)
 
     drain(q_all.at[pl.ds(0, tokens - tok), pl.ds(0, HD)], q_s)
+    drain(mixed.at[pl.ds(0, tokens - tok)], o_s)
     drain(v_all.at[pl.ds(0, tokens - tok)], v_s)
     drain(others, az_s)
     drain(other_lines, cz_s)

time: 92.9 us -> 91.6 us (0.986)
  Pallas kernels: 91.4 us -> 90.2 us
    pallas_call x1, Pallas kernels: 89.4 us -> 88.2 us  [per_device(): pl.pallas_call(functools.partial(step_kernel, (tok, groups, nz, ny)), nam...]
where the time goes in v4:
time: 91.6 us; the launch traced here: 91.5 us
  Pallas kernels  90.2 us (98%)
  between operations  1.29 us (1%)
    pallas_call x1, Pallas kernels, per_device(): pl.pallas_call(functools.partial(step_kernel, (tok, groups, nz, ny)), nam...  88.2 us
    pallas_call x1, Pallas kernels, per_device(): pl.pallas_call(adamw_kernel, name='adamw', out_shape=[jax.ShapeDtypeStruc...  1.99 us

profile of v4, /device:TPU:6, one launch (start us, length us, event | category | flops | bytes accessed | tf_op | source)
XLA Modules:
  0.0 91.5 jit_solution(6942090140712542801)
XLA Ops:
  1.3 88.2 %adapter_step.1 = (f32[128,128]{1,0:T(8,128)}, f32[8,3072]{1,0:T(8,128)}) custom-call(s32[1]{0:T(128)S(6)} %copy.18.count_ref, s32[1,3]{1,0:T(1,128)} %lengths_ref.1, bf16[1,192,2048]{2,1,0:T(8,128)(2,1)} %q_hbm.1, bf16[1,192,2048]{2,1,0:T(8,128)(2,1)} %k_hbm.1, bf16[1,192,2048]{2,1,0:T(8,128)(2,1)} %v_hbm.1, bf16[1,192,3072]{2,1,0:T(8,128)(2,1)} %og_hbm.1, ...), custom_call_target="tpu_custom_call" | custom-call | tf_op jit(solution)/shard_map/adapter_step/pallas_call | solution.py:729
  89.5 2.0 %adamw.1 = (f32[128,128]{1,0:T(8,128)}, f32[128,128]{1,0:T(8,128)}, f32[128,128]{1,0:T(8,128)}, f32[8,3072]{1,0:T(8,128)}, f32[8,3072]{1,0:T(8,128)}, /*index=5*/f32[8,3072]{1,0:T(8,128)}) custom-call(f32[128,128]{1,0:T(8,128)} %refs_0_.1, f32[128,128]{1,0:T(8,128)} %get-tuple-element.8.refs_1_, f32[128,128]{1,0:T(8,128)} %refs_2_.1, f32[128,128]{1,0:T(8,128)} %refs_3_.1, ...), custom_call_target="tpu_custom_call" | custom-call | tf_op jit(solution)/shard_map/adamw/pallas_call | solution.py:786

commit v5 on v4

--- a/solution.py
+++ b/solution.py
@@ -21,8 +21,8 @@
 EXP2_SCALE = HD ** (-0.5) * math.log2(math.e)
 MASK = -131072.0
 KEY_CHUNKS = 4
-EARLY_CHIPS = 5
-MORE = 3
+EARLY_CHIPS = 6
+MORE = 4
 ROWS = 64
 
 
@@ -461,11 +461,13 @@
 
     each(chips // 2 - 1, two_blocks)
     make_slopes()
-    spread_slopes()
     wait_queries(chips - 1)
     scores(chips - 1, 1)
     weigh(chips - 2, 0)
     weigh(chips - 1, 1)
+
+    drain(v_all.at[pl.ds(0, tokens - tok)], v_s)
+    spread_slopes()
 
     def mix_block(i):
         mix(i)
@@ -653,7 +655,6 @@
 
     drain(q_all.at[pl.ds(0, tokens - tok), pl.ds(0, HD)], q_s)
     drain(mixed.at[pl.ds(0, tokens - tok)], o_s)
-    drain(v_all.at[pl.ds(0, tokens - tok)], v_s)
     drain(others, az_s)
     drain(other_lines, cz_s)
     drain(slopes_all.at[pl.ds(0, chips * tok)], sl_s)

time: 91.6 us -> 92.6 us (1.011)
  no operation moved by 1% of the time
where the time goes in v5:
time: 92.6 us; the launch traced here: 92.4 us
  Pallas kernels  91.1 us (98%)
  between operations  1.29 us (1%)
    pallas_call x1, Pallas kernels, per_device(): pl.pallas_call(functools.partial(step_kernel, (tok, groups, nz, ny)), nam...  89.1 us
    pallas_call x1, Pallas kernels, per_device(): pl.pallas_call(adamw_kernel, name='adamw', out_shape=[jax.ShapeDtypeStruc...  1.99 us

profile of v5, /device:TPU:6, one launch (start us, length us, event | category | flops | bytes accessed | tf_op | source)
XLA Modules:
  0.0 92.4 jit_solution(18053193975152119132)
XLA Ops:
  1.3 89.1 %adapter_step.1 = (f32[128,128]{1,0:T(8,128)}, f32[8,3072]{1,0:T(8,128)}) custom-call(s32[1]{0:T(128)S(6)} %copy.18.count_ref, s32[1,3]{1,0:T(1,128)} %lengths_ref.1, bf16[1,192,2048]{2,1,0:T(8,128)(2,1)} %q_hbm.1, bf16[1,192,2048]{2,1,0:T(8,128)(2,1)} %k_hbm.1, bf16[1,192,2048]{2,1,0:T(8,128)(2,1)} %v_hbm.1, bf16[1,192,3072]{2,1,0:T(8,128)(2,1)} %og_hbm.1, ...), custom_call_target="tpu_custom_call" | custom-call | tf_op jit(solution)/shard_map/adapter_step/pallas_call | solution.py:730
  90.4 2.0 %adamw.1 = (f32[128,128]{1,0:T(8,128)}, f32[128,128]{1,0:T(8,128)}, f32[128,128]{1,0:T(8,128)}, f32[8,3072]{1,0:T(8,128)}, f32[8,3072]{1,0:T(8,128)}, /*index=5*/f32[8,3072]{1,0:T(8,128)}) custom-call(f32[128,128]{1,0:T(8,128)} %refs_0_.1, f32[128,128]{1,0:T(8,128)} %get-tuple-element.8.refs_1_, f32[128,128]{1,0:T(8,128)} %refs_2_.1, f32[128,128]{1,0:T(8,128)} %refs_3_.1, ...), custom_call_target="tpu_custom_call" | custom-call | tf_op jit(solution)/shard_map/adamw/pallas_call | solution.py:787
